TPU v7x, 256 devices: a whole 4x4x8 slice. The times are simulated.
256 devices in a mesh: prow: 32 (over y, x, core), pcol: 8 (over z).
Axes of the slice: x: 4, y: 4, z: 8, core: 2. Of those that a mesh axis runs over, the one named last changes fastest.
Arguments:
- designs: float32 [8192, 64], P('prow'), may hold values from -4 to 4
- length_weights: float32 [64], replicated, may hold values from 0.002 to 0.03
- trailing: float32 [16384, 16384], P('prow', 'pcol'), as said below
Outputs:
- updated_trailing: float32 [16384, 16384], P('prow', 'pcol')
- panel_rows: float32 [16384, 512], P('prow', 'pcol')
- panel_factor: float32 [512, 512], P(None, 'pcol')
Inputs may be any that keep to these rules, and one draw needn't show every extreme that they name: `trailing`: symmetric.
All inputs are finite; a program needn't handle non-finite values.
Results may differ from a plain program's by a relative error of at most 0.0003.
Values sent between devices are 32-bit elements; how exact they have to be, the bound alone decides.
No kernel may reach another device: no remote copies, remote signals or barrier semaphores. Data moves between devices by JAX's collectives and lax.ppermute only.
A program may use at most 128 MiB of HBM per device.

v0:
```python
import math

import jax
import jax.numpy as jnp
from jax import lax
from jax.sharding import PartitionSpec as P

PANEL = 512
DESIGNS = 8192


signal_variance = 4.0
nugget_level = 0.1


def broadcast(block, axis, holder):
    block = jnp.where(lax.axis_index(axis) == holder, block, jnp.zeros_like(block))
    return lax.psum(block, axis)


def scaled_pair(row_points, panel_points, length_weights):
    root_weights = jnp.sqrt(length_weights)
    return (row_points * root_weights, panel_points * root_weights)


def kernel_values(scaled_rows, scaled_panel):
    inner_terms = jnp.dot(scaled_rows, scaled_panel.T, precision=lax.Precision.HIGHEST)
    squares_rows = jnp.sum(scaled_rows * scaled_rows, axis=1)[:, None]
    squares_panel = jnp.sum(scaled_panel * scaled_panel, axis=1)[None, :]
    return signal_variance * jnp.exp(-(squares_rows + squares_panel - 2.0 * inner_terms))


def cross_block(row_points, panel_points, length_weights):
    scaled_rows, scaled_panel = scaled_pair(row_points, panel_points, length_weights)
    kernel = kernel_values(scaled_rows, scaled_panel)
    panel_gap = scaled_rows[:, -2][:, None] - scaled_panel[:, -2][None, :]
    trail_gap = scaled_rows[:, -1][:, None] - scaled_panel[:, -1][None, :]
    derivative_rows = -2.0 * kernel * trail_gap * panel_gap
    value_rows = math.sqrt(2.0) * kernel * panel_gap
    stacked = jnp.stack([derivative_rows, value_rows], axis=1)
    return stacked.reshape(2 * row_points.shape[0], panel_points.shape[0])


def diagonal_block(row_points, panel_points, length_weights, offset):
    scaled_rows, scaled_panel = scaled_pair(row_points, panel_points, length_weights)
    kernel = kernel_values(scaled_rows, scaled_panel)
    panel_gap = scaled_rows[:, -2][:, None] - scaled_panel[:, -2][None, :]
    row_iota = lax.broadcasted_iota(jnp.int32, kernel.shape, 0)
    col_iota = lax.broadcasted_iota(jnp.int32, kernel.shape, 1) + offset
    return kernel * (1.0 - 2.0 * panel_gap * panel_gap) + jnp.where(
        row_iota == col_iota, nugget_level, 0.0
    )


def right_solve(factor, matrix):
    return jax.scipy.linalg.solve_triangular(factor, matrix.T, lower=True).T


def body(designs, length_weights, trailing):
    per_device = designs.shape[0]
    grid_rows = lax.axis_size("prow")
    grid_cols = lax.axis_size("pcol")
    col_index = lax.axis_index("pcol")
    first_holder = (DESIGNS - PANEL) // per_device
    gathered = [broadcast(designs, "prow", holder) for holder in range(first_holder, grid_rows)]
    panel_points = jnp.concatenate(gathered, 0)
    block_width = PANEL // grid_cols
    column_points = lax.dynamic_slice_in_dim(panel_points, col_index * block_width, block_width, 0)
    column_offset = col_index * block_width
    block = jnp.concatenate(
        [
            diagonal_block(panel_points, column_points, length_weights, column_offset),
            cross_block(designs, column_points, length_weights),
        ],
        0,
    )
    row_iota = lax.broadcasted_iota(jnp.int32, block.shape, 0)
    factor_columns = []
    for column_step in range(grid_cols):
        owner_here = col_index == column_step
        diag_part = block[column_step * block_width : (column_step + 1) * block_width]
        diag_part = jnp.where(owner_here, diag_part, jnp.eye(block_width, dtype=jnp.float32))
        diag_factor = jnp.linalg.cholesky(diag_part)
        candidate = right_solve(diag_factor, block)
        candidate = jnp.where(row_iota < column_step * block_width, 0.0, candidate)
        received = broadcast(candidate, "pcol", column_step)
        factor_columns.append(received)
        own_rows = lax.dynamic_slice_in_dim(received, column_offset, block_width, 0)
        reduced = block - jnp.dot(received, own_rows.T, precision=lax.Precision.HIGHEST)
        block = jnp.where(col_index > column_step, reduced, block)
    full_factor = jnp.concatenate(factor_columns, 1)
    panel_factor = full_factor[:PANEL]
    row_factor = full_factor[PANEL:]
    local_rows = row_factor.shape[0]
    row_share = grid_rows // grid_cols
    updated_pieces = []
    for part_step in range(row_share):
        holder_index = col_index * row_share + part_step
        far_rows = broadcast(row_factor, "prow", holder_index)
        trailing_part = trailing[:, part_step * local_rows : (part_step + 1) * local_rows]
        updated_pieces.append(
            trailing_part - jnp.dot(row_factor, far_rows.T, precision=lax.Precision.HIGHEST)
        )
    updated = jnp.concatenate(updated_pieces, 1)
    rows_shard = lax.dynamic_slice_in_dim(row_factor, col_index * block_width, block_width, 1)
    factor_shard = lax.dynamic_slice_in_dim(panel_factor, col_index * block_width, block_width, 1)
    return (updated, rows_shard, factor_shard)


def solution(mesh):
    in_specs = (P("prow", None), P(), P("prow", "pcol"))
    out_specs = (P("prow", "pcol"), P("prow", "pcol"), P(None, "pcol"))
    return jax.shard_map(body, mesh=mesh, in_specs=in_specs, out_specs=out_specs, check_vma=False)
```

profile of v0, /device:TPU:65, one launch (start us, length us, event | category | flops | bytes accessed | tf_op | source)
XLA Modules:
  0.0 962.4 jit_solution(14459072166628240540)
XLA Ops:
  7.2 0.7 sqrt.4
  7.9 1.5 broadcast_select_fusion.4
  9.5 114.5 %all-reduce.31.cloned.1.call-done = (f32[256,64]{0,1:T(8,128)}, f32[256,64]{0,1:T(8,128)}) async-done(((f32[256,64]{0,1:T(8,128)}, f32[256,64]{0,1:T(8,128)}), (f32[256,64]{0,1:T(8,128)}, f32[256,64]{0,1:T(8,128)})) %all-reduce.31.cloned.1.call-update) | async-done | bytes 131088 | tf_op jit(solution)/shard_map/psum | solution.py:18
  124.0 0.8 constant_dynamic-update-slice_fusion.1
  124.9 0.8 constant_dynamic-update-slice_fusion
  126.4 5.8 cholesky.134
  133.6 4.9 custom-call.12
  139.1 1.1 fusion.21
  140.3 66.4 %all-reduce.13.cloned.1.call-done = f32[1024,64]{0,1:T(8,128)} async-done(((f32[1024,64]{0,1:T(8,128)}), f32[1024,64]{0,1:T(8,128)}) %all-reduce.13.cloned.1.call-update) | async-done | bytes 262160 | tf_op jit(solution)/shard_map/psum | solution.py:18
  206.7 1.4 fusion.20
  208.3 5.9 cholesky.145
  214.9 0.7 fusion.43
  215.5 4.9 custom-call.13
  220.4 1.1 fusion.19
  221.7 71.0 %all-reduce.15.cloned.1.call-done = f32[1024,64]{0,1:T(8,128)} async-done(((f32[1024,64]{0,1:T(8,128)}), f32[1024,64]{0,1:T(8,128)}) %all-reduce.15.cloned.1.call-update) | async-done | bytes 262160 | tf_op jit(solution)/shard_map/psum | solution.py:18
  292.7 1.4 fusion.17
  294.2 5.8 cholesky.156
  300.8 0.7 fusion.44
  301.4 4.9 custom-call.14
  306.3 1.1 fusion.16
  307.5 71.0 %all-reduce.17.cloned.1.call-done = f32[1024,64]{0,1:T(8,128)} async-done(((f32[1024,64]{0,1:T(8,128)}), f32[1024,64]{0,1:T(8,128)}) %all-reduce.17.cloned.1.call-update) | async-done | bytes 262160 | tf_op jit(solution)/shard_map/psum | solution.py:18
  378.5 1.4 fusion.14
  380.2 5.9 cholesky.167
  387.4 4.9 custom-call.15
  392.3 1.1 fusion.13
  393.7 70.8 %all-reduce.19.cloned.1.call-done = f32[1024,64]{0,1:T(8,128)} async-done(((f32[1024,64]{0,1:T(8,128)}), f32[1024,64]{0,1:T(8,128)}) %all-reduce.19.cloned.1.call-update) | async-done | bytes 262160 | tf_op jit(solution)/shard_map/psum | solution.py:18
  464.5 1.4 fusion.11
  466.1 5.8 cholesky.178
  472.6 0.7 fusion.46
  473.3 4.9 custom-call.16
  478.2 1.1 fusion.10
  479.4 71.0 %all-reduce.21.cloned.1.call-done = f32[1024,64]{0,1:T(8,128)} async-done(((f32[1024,64]{0,1:T(8,128)}), f32[1024,64]{0,1:T(8,128)}) %all-reduce.21.cloned.1.call-update) | async-done | bytes 262160 | tf_op jit(solution)/shard_map/psum | solution.py:18
  550.4 1.4 fusion.8
  552.1 5.9 cholesky.189
  559.3 4.9 custom-call.17
  564.2 1.1 fusion.7
  565.5 70.9 %all-reduce.23.cloned.1.call-done = f32[1024,64]{0,1:T(8,128)} async-done(((f32[1024,64]{0,1:T(8,128)}), f32[1024,64]{0,1:T(8,128)}) %all-reduce.23.cloned.1.call-update) | async-done | bytes 262160 | tf_op jit(solution)/shard_map/psum | solution.py:18
  636.4 1.4 fusion.5
  637.9 5.8 cholesky.200
  645.1 4.9 custom-call.18
  650.0 1.1 fusion.4
  651.3 1.0 constant_dynamic-update-slice_fusion.6
  652.3 69.9 %all-reduce.25.cloned.1.call-done = f32[1024,64]{0,1:T(8,128)} async-done(((f32[1024,64]{0,1:T(8,128)}), f32[1024,64]{0,1:T(8,128)}) %all-reduce.25.cloned.1.call-update) | async-done | bytes 262160 | tf_op jit(solution)/shard_map/psum | solution.py:18
  722.2 1.5 fusion.2
  724.0 5.9 cholesky.211
  731.2 4.9 custom-call.19
  736.1 1.1 fusion.1
  737.5 1.0 constant_dynamic-update-slice_fusion.4
  738.5 69.8 %all-reduce.27.cloned.1.call-done = f32[1024,64]{0,1:T(8,128)} async-done(((f32[1024,64]{0,1:T(8,128)}), f32[1024,64]{0,1:T(8,128)}) %all-reduce.27.cloned.1.call-update) | async-done | bytes 262160 | tf_op jit(solution)/shard_map/psum | solution.py:18
  808.3 1.0 constant_dynamic-update-slice_fusion.2
  809.3 3.0 fusion.86
  812.4 4.0 fusion.85
  816.3 2.5 copy.35
  818.9 2.5 copy.36
  821.4 1.3 copy.37
  822.7 1.6 copy.38
  824.3 1.7 constant_dynamic-slice_fusion
  826.0 112.6 %all-reduce.29.cloned.1.call-done = (f32[512,512]{0,1:T(8,128)}, f32[512,512]{0,1:T(8,128)}, f32[512,512]{0,1:T(8,128)}, f32[512,512]{0,1:T(8,128)}) async-done(((f32[512,512]{0,1:T(8,128)}, f32[512,512]{0,1:T(8,128)}, f32[512,512]{0,1:T(8,128)}, f32[512,512]{0,1:T(8,128)}), (f32[512,512]{0,1:T(8,128)}, f32[512,512]{0,1:T(8,128)}, f32[512,512]{0,1:T(8,128)}, ...) | async-done | bytes 4194320 | tf_op jit(solution)/shard_map/psum | solution.py:18
  938.5 3.6 convolution_subtract_fusion.3
  942.1 1.9 convolution_subtract_fusion.2
  944.0 1.9 convolution_subtract_fusion.1
  945.9 1.9 convolution_subtract_fusion
  947.8 2.4 pad_maximum_fusion
  950.2 5.3 copy.34
  (108 shorter events, 12.3 us)
Async XLA Ops:
  7.2 116.8 %all-reduce.31.cloned.1.call-start = ((), (), s32[]{:S(2)}) async-start(), calls=%async_computation.9 | async-start | bytes 262144 | tf_op jit(solution)/shard_map/psum | solution.py:18
  9.4 197.2 %all-reduce.13.cloned.1.call-start = ((), (), s32[]{:S(2)}) async-start(), calls=%async_computation | async-start | bytes 524288 | tf_op jit(solution)/shard_map/psum | solution.py:18
  140.2 152.5 %all-reduce.15.cloned.1.call-start = ((), (), s32[]{:S(2)}) async-start(), calls=%async_computation.1 | async-start | bytes 524288 | tf_op jit(solution)/shard_map/psum | solution.py:18
  221.6 156.9 %all-reduce.17.cloned.1.call-start = ((), (), s32[]{:S(2)}) async-start(), calls=%async_computation.2 | async-start | bytes 524288 | tf_op jit(solution)/shard_map/psum | solution.py:18
  307.5 157.1 %all-reduce.19.cloned.1.call-start = ((), (), s32[]{:S(2)}) async-start(), calls=%async_computation.3 | async-start | bytes 524288 | tf_op jit(solution)/shard_map/psum | solution.py:18
  393.5 172.0 %copy-start.2 = (f32[1024,64]{0,1:T(8,128)S(1)}, f32[1024,64]{0,1:T(8,128)}, u32[]{:S(2)}) copy-start(f32[1024,64]{0,1:T(8,128)} %all-reduce.13.cloned.1.call-done) | copy-start | bytes 786436
  393.5 156.9 %all-reduce.21.cloned.1.call-start = ((), (), s32[]{:S(2)}) async-start(), calls=%async_computation.4 | async-start | bytes 524288 | tf_op jit(solution)/shard_map/psum | solution.py:18
  479.3 157.0 %all-reduce.23.cloned.1.call-start = ((), (), s32[]{:S(2)}) async-start(), calls=%async_computation.5 | async-start | bytes 524288 | tf_op jit(solution)/shard_map/psum | solution.py:18
  479.4 171.8 %copy-start.3 = (f32[1024,64]{0,1:T(8,128)S(1)}, f32[1024,64]{0,1:T(8,128)}, u32[]{:S(2)}) copy-start(f32[1024,64]{0,1:T(8,128)} %all-reduce.15.cloned.1.call-done) | copy-start | bytes 786436
  551.8 99.5 %copy-start.4 = (f32[1024,64]{0,1:T(8,128)S(1)}, f32[1024,64]{0,1:T(8,128)}, u32[]{:S(2)}) copy-start(f32[1024,64]{0,1:T(8,128)} %all-reduce.17.cloned.1.call-done) | copy-start | bytes 786436
  565.3 156.9 %all-reduce.25.cloned.1.call-start = ((), (), s32[]{:S(2)}) async-start(), calls=%async_computation.6 | async-start | bytes 524288 | tf_op jit(solution)/shard_map/psum | solution.py:18
  650.0 87.5 %copy-start.5 = (f32[1024,64]{0,1:T(8,128)S(1)}, f32[1024,64]{0,1:T(8,128)}, u32[]{:S(2)}) copy-start(f32[1024,64]{0,1:T(8,128)} %all-reduce.21.cloned.1.call-done) | copy-start | bytes 786436
  651.2 157.1 %all-reduce.27.cloned.1.call-start = ((), (), s32[]{:S(2)}) async-start(), calls=%async_computation.7 | async-start | bytes 524288 | tf_op jit(solution)/shard_map/psum | solution.py:18
  722.2 16.3 %copy-start.6 = (f32[1024,64]{0,1:T(8,128)S(1)}, f32[1024,64]{0,1:T(8,128)}, u32[]{:S(2)}) copy-start(f32[1024,64]{0,1:T(8,128)} %all-reduce.25.cloned.1.call-done) | copy-start | bytes 786436
  737.2 201.3 %all-reduce.29.cloned.1.call-start = ((), (), s32[]{:S(2)}) async-start(), calls=%async_computation.8 | async-start | bytes 8388608 | tf_op jit(solution)/shard_map/psum | solution.py:18
  938.5 3.6 copy-start.1
  938.5 3.6 copy-start.9
  942.1 1.9 copy-start
  942.1 1.9 copy-start.8
  944.0 1.9 copy-start.7
Sparse Core Ops, SparseCore 0:
  11.8 112.1 all-reduce.30
  140.3 66.2 all-reduce.12
  221.7 70.9 all-reduce.14
  307.6 70.8 all-reduce.16
  393.6 70.8 all-reduce.18
  479.5 70.8 all-reduce.20
  565.4 70.8 all-reduce.22
  651.3 70.8 all-reduce.24
  737.4 70.9 all-reduce.26
  812.5 126.0 all-reduce.28
where the time goes:
time: 965 us; the launch traced here: 962 us
  waiting for transfers between devices  788 us (82%)
  other arithmetic  104 us (11%)
  matrix products  29 us (3%)
  local copies, waits for them, and re-layouts  25.2 us (3%)
  between operations  14.8 us (2%)
    psum x10, waiting for transfers between devices, broadcast(): return lax.psum(block, axis)  788 us
    another operation x24, other arithmetic, body(): diag_factor = jnp.linalg.cholesky(diag_part)  52.2 us
    another operation x16, other arithmetic, right_solve(): return jax.scipy.linalg.solve_triangular(factor, matrix.T, lower=True).T  44.4 us
  transfers between devices with their start and end apart: 10, of which 10 were waited for; matrix products, arithmetic and copies ran while one was open for 2% of the time, Pallas kernels for 0%

commit v1 on v0

v1 whole, which is shorter than its diff:
```python
import math

import jax
import jax.numpy as jnp
from jax import lax
from jax.experimental import pallas as pl
from jax.experimental.pallas import tpu as pltpu
from jax.sharding import PartitionSpec as P

PANEL = 512
DIM = 64
BLOCK = 128
GROUP = 8

signal_variance = 4.0
nugget_level = 0.1

F32 = jnp.float32
BF16 = jnp.bfloat16
HIGHEST = lax.Precision.HIGHEST
NT = (((1,), (1,)), ((), ()))
NN = (((1,), (0,)), ((), ()))


def dot_nt(a, b):
    return lax.dot_general(a, b, NT, precision=HIGHEST, preferred_element_type=F32)


def dot_nn(a, b):
    return lax.dot_general(a, b, NN, precision=HIGHEST, preferred_element_type=F32)


def split(x):
    hi = x.astype(BF16)
    return hi, (x - hi.astype(F32)).astype(BF16)


def dot_split(a, b):
    one = lambda p, q: lax.dot_general(p, q, NT, preferred_element_type=F32)
    return one(a[0], b[0]) + (one(a[0], b[1]) + one(a[1], b[0]))


def lane_spread(x, lane):
    return jnp.broadcast_to(x[:, lane : lane + 1], (8, 128))


def row_spread(x, row):
    return jnp.broadcast_to(x[row : row + 1, :], (8, 128))


def factor_block(rows):
    lane = lax.broadcasted_iota(jnp.int32, (8, 128), 1)
    sub = lax.broadcasted_iota(jnp.int32, (8, 128), 0)
    rows = list(rows)
    for g in range(len(rows)):
        base = GROUP * g
        slab = rows[g]
        cols = [lane_spread(slab, base + j) for j in range(GROUP)]
        s = [[row_spread(cols[j], k) if k <= j else None for j in range(GROUP)] for k in range(GROUP)]
        r = [None] * GROUP
        u = [[None] * GROUP for _ in range(GROUP)]
        for k in range(GROUP):
            r[k] = lax.rsqrt(s[k][k])
            for j in range(k + 1, GROUP):
                u[k][j] = s[k][j] * r[k]
            for i in range(k + 1, GROUP):
                for j in range(i, GROUP):
                    s[i][j] = s[i][j] - u[k][i] * u[k][j]
        pivots = []
        final = slab
        for k in range(GROUP):
            row = row_spread(slab, k)
            for m in range(k):
                row = row - u[m][k] * pivots[m]
            row = row * r[k]
            diag = lane == base + k
            final = jnp.where(sub == k, jnp.where(diag, r[k], row), final)
            pivots.append(jnp.where(diag, s[k][k] * r[k] + r[k], row))
        rows[g] = final
        for i in range(g + 1, len(rows)):
            x = rows[i]
            c = [lane_spread(x, base + j) for j in range(GROUP)]
            for k in range(GROUP):
                low = c[k] * r[k]
                for j in range(k + 1, GROUP):
                    c[j] = c[j] - low * u[k][j]
                x = x - low * pivots[k]
            rows[i] = x
    return rows


def row_forms(points):
    shape = (8, DIM)
    sub = lax.broadcasted_iota(jnp.int32, shape, 0)
    lane = lax.broadcasted_iota(jnp.int32, shape, 1)
    pick = jnp.where(lane == DIM - 2 + sub, 1.0, 0.0).astype(F32)
    picked = dot_nt(pick, points)
    squares = dot_nt(jnp.ones(shape, F32), points * points)
    return squares[0:1], picked[0:1], picked[1:2]


def kernel_values(rows, points, squares_points):
    squares_rows = jnp.sum(rows * rows, axis=1, keepdims=True)
    gaps = squares_rows + squares_points - 2.0 * dot_nt(rows, points)
    return signal_variance * jnp.exp(-gaps)


def factor_kernel(panel_ref, weights_ref, factor_ref, inverse_ref, work_ref, block_ref):
    points = panel_ref[...] * jnp.sqrt(weights_ref[...])
    squares, along_u, _ = row_forms(points)
    kernel = kernel_values(points, points, squares)
    gap = points[:, DIM - 2 : DIM - 1] - along_u
    row_iota = lax.broadcasted_iota(jnp.int32, (PANEL, PANEL), 0)
    col_iota = lax.broadcasted_iota(jnp.int32, (PANEL, PANEL), 1)
    work_ref[...] = kernel * (1.0 - 2.0 * gap * gap) + jnp.where(row_iota == col_iota, nugget_level, 0.0)
    factor_ref[...] = jnp.zeros_like(factor_ref)
    inverse_ref[...] = jnp.zeros_like(inverse_ref)

    @pl.loop(0, PANEL // BLOCK)
    def _(step):
        at = pl.multiple_of(step * BLOCK, BLOCK)
        rows = [work_ref[pl.ds(at + 8 * i, 8), pl.ds(at, BLOCK)] for i in range(BLOCK // 8)]
        rows = factor_block(rows)
        for i in range(BLOCK // 8):
            block_ref[8 * i : 8 * i + 8, :] = rows[i]
        both = block_ref[...]
        r = lax.broadcasted_iota(jnp.int32, (BLOCK, BLOCK), 0)
        c = lax.broadcasted_iota(jnp.int32, (BLOCK, BLOCK), 1)
        upper = jnp.where(c > r, both, jnp.where(c == r, 1.0 / both, 0.0))
        factor_ref[pl.ds(at, BLOCK), pl.ds(at, BLOCK)] = upper.T
        inverse = jnp.where(c <= r, both, 0.0)
        inverse_ref[pl.ds(at, BLOCK), pl.ds(at, BLOCK)] = inverse
        for s in range(PANEL // BLOCK - 1):

            @pl.when(step == s)
            def _():
                end = BLOCK * (s + 1)
                below = dot_nt(work_ref[end:, end - BLOCK : end], inverse)
                factor_ref[end:, end - BLOCK : end] = below
                work_ref[end:, end:] = work_ref[end:, end:] - dot_nt(below, below)

    for n in (BLOCK, 2 * BLOCK):
        for t in range(0, PANEL, 2 * n):
            left = dot_nn(factor_ref[t + n : t + 2 * n, t : t + n], inverse_ref[t : t + n, t : t + n])
            inverse_ref[t + n : t + 2 * n, t : t + n] = -dot_nn(
                inverse_ref[t + n : t + 2 * n, t + n : t + 2 * n], left
            )


def factor_call(panel_points, weights):
    square = jax.ShapeDtypeStruct((PANEL, PANEL), F32)
    return pl.pallas_call(
        factor_kernel,
        out_shape=[square, square],
        scratch_shapes=[pltpu.VMEM((PANEL, PANEL), F32), pltpu.VMEM((BLOCK, BLOCK), F32)],
        compiler_params=pltpu.CompilerParams(vmem_limit_bytes=32 << 20),
        name="panel_factor",
    )(panel_points, weights)


def solved_rows(designs, weights, points, squares, along_u, along_v, inverse, cross_ref):
    rows = designs * jnp.sqrt(weights)
    kernel = kernel_values(rows, points, squares)
    gap_u = rows[:, DIM - 2 : DIM - 1] - along_u
    gap_v = rows[:, DIM - 1 : DIM] - along_v
    n = designs.shape[0]
    derivative = -2.0 * kernel * gap_v * gap_u
    value = math.sqrt(2.0) * kernel * gap_u
    for q in range(PANEL // 128):
        cross_ref[q, pl.ds(0, n, stride=2), :] = derivative[:, 128 * q : 128 * q + 128]
        cross_ref[q, pl.ds(1, n, stride=2), :] = value[:, 128 * q : 128 * q + 128]
    cross = jnp.concatenate([cross_ref[q] for q in range(PANEL // 128)], 1)
    return dot_split(split(cross), inverse)


def update_kernel(
    own_ref, far_ref, panel_ref, weights_ref, inverse_ref, trailing_ref,
    updated_ref, rows_ref, points_ref, forms_ref, inv_hi_ref, inv_lo_ref, row_hi_ref, row_lo_ref, cross_ref,
):
    weights = weights_ref[...]

    def solve(designs):
        forms = forms_ref[...]
        return solved_rows(
            designs, weights, points_ref[...], forms[0:1], forms[1:2], forms[2:3],
            (inv_hi_ref[...], inv_lo_ref[...]), cross_ref,
        )

    @pl.when(pl.program_id(0) == 0)
    def _():
        points = panel_ref[...] * jnp.sqrt(weights)
        points_ref[...] = points
        squares, along_u, along_v = row_forms(points)
        forms_ref[0:1, :] = squares
        forms_ref[1:2, :] = along_u
        forms_ref[2:3, :] = along_v
        hi, lo = split(inverse_ref[...])
        inv_hi_ref[...] = hi
        inv_lo_ref[...] = lo
        own = solve(own_ref[...])
        rows_ref[...] = own
        hi, lo = split(own)
        row_hi_ref[...] = hi
        row_lo_ref[...] = lo

    far = split(solve(far_ref[...]))
    updated_ref[...] = trailing_ref[...] - dot_split((row_hi_ref[...], row_lo_ref[...]), far)


def update_call(designs, far_designs, panel_points, weights, inverse, trailing):
    n = designs.shape[0]
    height, width = trailing.shape
    steps = far_designs.shape[0] // n
    whole = lambda *shape: pl.BlockSpec(shape, lambda j: (0,) * len(shape))
    tile = pl.BlockSpec((height, width // steps), lambda j: (0, j))
    return pl.pallas_call(
        update_kernel,
        grid=(steps,),
        in_specs=[
            whole(n, DIM), pl.BlockSpec((n, DIM), lambda j: (j, 0)), whole(PANEL, DIM), whole(1, DIM),
            whole(PANEL, PANEL), tile,
        ],
        out_specs=[tile, whole(height, PANEL)],
        out_shape=[jax.ShapeDtypeStruct((height, width), F32), jax.ShapeDtypeStruct((height, PANEL), F32)],
        scratch_shapes=[
            pltpu.VMEM((PANEL, DIM), F32), pltpu.VMEM((8, PANEL), F32), pltpu.VMEM((PANEL, PANEL), BF16),
            pltpu.VMEM((PANEL, PANEL), BF16), pltpu.VMEM((height, PANEL), BF16), pltpu.VMEM((height, PANEL), BF16),
            pltpu.VMEM((PANEL // 128, 2 * n, 128), F32),
        ],
        compiler_params=pltpu.CompilerParams(vmem_limit_bytes=48 << 20, dimension_semantics=("arbitrary",)),
        name="trailing_update",
    )(designs, far_designs, panel_points, weights, inverse, trailing)


NY, NX, NC = 4, 4, 2
DEVICES = NY * NX * NC


def place(y, x, core):
    return (y * NX + x) * NC + core


def pairs_of(grid_cols, moves):
    return [(a * grid_cols + c, b * grid_cols + c) for c in range(grid_cols) for a, b in moves(c)]


def gather_designs(designs, grid_cols):
    axes = ("prow", "pcol")
    at = lax.axis_index("prow")
    col = lax.axis_index("pcol")
    x_at, y_at, core = at // NC % NX, at // (NX * NC), at % NC
    cores, xs, ys = range(NC), range(NX), range(NY)
    send = lambda block, moves: lax.ppermute(block, axes, pairs_of(grid_cols, moves))

    from_x = [designs] + [
        lax.ppermute(designs, "prow", [(place(y, x, c), place(y, (x + s) % NX, c)) for y in ys for x in xs for c in cores])
        for s in range(1, NX)
    ]

    def block_of(x):
        shift = (x_at - x) % NX
        block = from_x[0]
        for s in range(1, NX):
            block = jnp.where(shift == s, from_x[s], block)
        return block

    panel = block_of(NX - 1)
    got = [send(panel, lambda _: [(place(NY - 1, x, c), place(t, x, c)) for x in xs for c in cores]) for t in range(NY - 1)]
    for t in range(NY - 1):
        panel = jnp.where(y_at == t, got[t], panel)
    other = lax.ppermute(panel, "prow", [(j, j ^ 1) for j in range(DEVICES)])
    panel_points = jnp.where(core == 0, jnp.concatenate([panel, other], 0), jnp.concatenate([other, panel], 0))

    half = 2 * (col % 2)
    far = jnp.stack([block_of(half), block_of(half + 1)], 0)
    got = [
        send(far, lambda z: [(place(z // 2, x, c), place((z // 2 + s) % NY, x, c)) for x in xs for c in cores])
        for s in range(1, NY)
    ]
    for s in range(1, NY):
        far = jnp.where((y_at - col // 2) % NY == s, got[s - 1], far)
    other = lax.ppermute(far, "prow", [(j, j ^ 1) for j in range(DEVICES)])
    first = jnp.where(core == 0, far, other)
    second = jnp.where(core == 0, other, far)
    far_designs = jnp.stack([first, second], 1).reshape(-1, DIM)
    return panel_points, far_designs


def body(designs, length_weights, trailing):
    grid_cols = lax.axis_size("pcol")
    col_index = lax.axis_index("pcol")
    weights = length_weights.reshape(1, DIM)
    panel_points, far_designs = gather_designs(designs, grid_cols)
    factor, inverse = factor_call(panel_points, weights)
    updated, rows = update_call(designs, far_designs, panel_points, weights, inverse, trailing)
    width = PANEL // grid_cols
    take = lambda whole: lax.dynamic_slice_in_dim(whole, col_index * width, width, 1)
    return updated, take(rows), take(factor)


def solution(mesh):
    in_specs = (P("prow", None), P(), P("prow", "pcol"))
    out_specs = (P("prow", "pcol"), P("prow", "pcol"), P(None, "pcol"))
    return jax.shard_map(body, mesh=mesh, in_specs=in_specs, out_specs=out_specs, check_vma=False)
```

time: 965 us -> 74.2 us (0.08)
  waiting for transfers between devices: 788 us -> 17.3 us
  other arithmetic: 104 us -> 0.26 us
  Pallas kernels: 0 us -> 36.9 us
  matrix products: 29 us -> 0 us
  local copies, waits for them, and re-layouts: 25.2 us -> 2.72 us
  starting transfers between devices: 0.82 us -> 16 us
  between operations: 14.8 us -> 0.79 us
    psum x10 -> x0, waiting for transfers between devices: 788 us -> none  [broadcast(): return lax.psum(block, axis)]
    another operation x41 -> x3, other arithmetic: 96.6 us -> 0.1 us  [the longest x2 0.08 us: gather_designs(): far_designs = jnp.stack([first, second], 1).reshape(-1, DIM)]
    pallas_call x0 -> x2, Pallas kernels: none -> 36.9 us  [the longest x1 21.8 us: factor_call(): pl.pallas_call(factor_kernel, out_shape=[square, square], scratch_shapes=...]
    dot_general x13 -> x0, matrix products: 20 us -> none  [the longest x7 10.1 us: body(): jnp.dot(received, own_rows.T, precision=lax.Precision.HIGHEST)]
    ppermute x0 -> x11, waiting for transfers between devices: none -> 17.3 us  [the longest x6 12.7 us: gather_designs(): lax.ppermute(block, axes, pairs_of(grid_cols, moves))]
    ppermute x0 -> x11, starting transfers between devices: none -> 16 us  [the longest x6 5.27 us: gather_designs(): lax.ppermute(block, axes, pairs_of(grid_cols, moves))]
    unnamed x33 -> x5, local copies, waits for them, and re-layouts: 16.2 us -> 2.49 us
  transfers between devices with their start and end apart: 10 -> 11, of which waited for: 10 -> 4; matrix products, arithmetic and copies ran while one was open for 2% -> 0% of each run, Pallas kernels for 0% -> 30%
where the time goes in v1:
time: 74.2 us; the launch traced here: 73.9 us
  Pallas kernels  36.9 us (50%)
  waiting for transfers between devices  17.3 us (23%)
  starting transfers between devices  16 us (22%)
  local copies, waits for them, and re-layouts  2.72 us (4%)
  between operations  0.79 us (1%)
    pallas_call x1, Pallas kernels, factor_call(): pl.pallas_call(factor_kernel, out_shape=[square, square], scratch_shapes=...  21.8 us
    pallas_call x1, Pallas kernels, update_call(): pl.pallas_call(update_kernel, grid=(steps,), in_specs=[whole(n, DIM), pl....  15.1 us
    ppermute x6, waiting for transfers between devices, gather_designs(): lax.ppermute(block, axes, pairs_of(grid_cols, moves))  12.7 us
    ppermute x6, starting transfers between devices, gather_designs(): lax.ppermute(block, axes, pairs_of(grid_cols, moves))  5.27 us
    ppermute x3, starting transfers between devices, gather_designs(): lax.ppermute(designs, 'prow', [(place(y, x, c), place(y, (x + s) % NX, c)...  4.89 us
    ppermute x3, waiting for transfers between devices, gather_designs(): lax.ppermute(designs, 'prow', [(place(y, x, c), place(y, (x + s) % NX, c)...  4.56 us
    ppermute x1, starting transfers between devices, gather_designs(): other = lax.ppermute(far, 'prow', [(j, j ^ 1) for j in range(DEVICES)])  3.02 us
    ppermute x1, starting transfers between devices, gather_designs(): other = lax.ppermute(panel, 'prow', [(j, j ^ 1) for j in range(DEVICES)])  2.78 us
  transfers between devices with their start and end apart: 11, of which 4 were waited for; matrix products, arithmetic and copies ran while one was open for 0% of the time, Pallas kernels for 30%

profile of v1, /device:TPU:65, one launch (start us, length us, event | category | flops | bytes accessed | tf_op | source)
XLA Modules:
  0.0 73.9 jit_solution(7897266067594937428)
XLA Ops:
  0.6 0.0 copy-start
  0.6 0.9 %copy.22.own_ref = f32[256,64]{1,0:T(8,128)S(1)} copy(f32[256,64]{0,1:T(8,128)} %param.3) | data formatting | bytes 131072 | tf_op args[0]
  1.6 1.3 %collective-permute-start.2 = (f32[256,64]{1,0:T(8,128)S(1)}, f32[256,64]{1,0:T(8,128)S(1)}, u32[]{:S(2)}, u32[]{:S(2)}) collective-permute-start(f32[256,64]{1,0:T(8,128)S(1)} %copy.22.own_ref), channel_id=1, source_target_pairs={{0,16},{8,24},{16,32},{24,40},{32,48},{40,56},{48,0},{56,8},{64,80... | collective-permute-start | bytes 196616 | tf_op jit(solution)/shard_map/ppermute | solution.py:256
  2.9 2.5 %collective-permute-start.1 = (f32[256,64]{1,0:T(8,128)S(1)}, f32[256,64]{1,0:T(8,128)S(1)}, u32[]{:S(2)}, u32[]{:S(2)}) collective-permute-start(f32[256,64]{1,0:T(8,128)S(1)} %copy.22.own_ref), channel_id=1, source_target_pairs={{0,32},{8,40},{16,48},{24,56},{32,0},{40,8},{48,16},{56,24},{64,96... | collective-permute-start | bytes 196616 | tf_op jit(solution)/shard_map/ppermute | solution.py:256
  5.3 1.2 %collective-permute-start = (f32[256,64]{1,0:T(8,128)S(1)}, f32[256,64]{1,0:T(8,128)S(1)}, u32[]{:S(2)}, u32[]{:S(2)}) collective-permute-start(f32[256,64]{1,0:T(8,128)S(1)} %copy.22.own_ref), channel_id=1, source_target_pairs={{0,48},{8,56},{16,0},{24,8},{32,16},{40,24},{48,32},{56,40},{64,11... | collective-permute-start | bytes 196616 | tf_op jit(solution)/shard_map/ppermute | solution.py:256
  6.5 0.8 %collective-permute-done.2 = f32[256,64]{1,0:T(8,128)S(1)} collective-permute-done((f32[256,64]{1,0:T(8,128)S(1)}, f32[256,64]{1,0:T(8,128)S(1)}, u32[]{:S(2)}, u32[]{:S(2)}) %collective-permute-start.2) | collective-permute-done | bytes 65568 | tf_op jit(solution)/shard_map/ppermute | solution.py:256
  7.2 3.8 %collective-permute-done.1 = f32[256,64]{1,0:T(8,128)S(1)} collective-permute-done((f32[256,64]{1,0:T(8,128)S(1)}, f32[256,64]{1,0:T(8,128)S(1)}, u32[]{:S(2)}, u32[]{:S(2)}) %collective-permute-start.1) | collective-permute-done | bytes 65568 | tf_op jit(solution)/shard_map/ppermute | solution.py:256
  11.0 0.0 collective-permute-done
  11.0 0.1 select_select_fusion.2
  11.1 1.3 %collective-permute-start.9 = (f32[256,64]{1,0:T(8,128)S(1)}, f32[256,64]{1,0:T(8,128)S(1)}, u32[]{:S(2)}, u32[]{:S(2)}) collective-permute-start(f32[256,64]{1,0:T(8,128)S(1)} %get-tuple-element.17), channel_id=1, source_target_pairs={{192,0},{200,8},{208,16},{216,24},{224,32},{232,40},{240,48},{248,... | collective-permute-start | bytes 196616 | tf_op jit(solution)/shard_map/ppermute | solution.py:253
  12.4 0.7 collective-permute-start.8
  13.1 0.7 collective-permute-start.7
  13.8 0.7 collective-permute-start.5
  14.5 0.7 collective-permute-start.4
  15.1 2.9 %collective-permute-done.9 = f32[256,64]{1,0:T(8,128)S(1)} collective-permute-done((f32[256,64]{1,0:T(8,128)S(1)}, f32[256,64]{1,0:T(8,128)S(1)}, u32[]{:S(2)}, u32[]{:S(2)}) %collective-permute-start.9) | collective-permute-done | bytes 65568 | tf_op jit(solution)/shard_map/ppermute | solution.py:253
  18.0 1.3 %collective-permute-start.3 = (f32[2,256,64]{2,1,0:T(8,128)S(1)}, f32[2,256,64]{2,1,0:T(8,128)S(1)}, u32[]{:S(2)}, u32[]{:S(2)}) collective-permute-start(f32[2,256,64]{2,1,0:T(8,128)S(1)} %pad_maximum_fusion.1), channel_id=1, source_target_pairs={{0,192},{8,200},{16,208},{24,216},{32,224},{40,232},{48,240},{56,2... | collective-permute-start | bytes 393224 | tf_op jit(solution)/shard_map/ppermute | solution.py:253
  19.3 0.0 collective-permute-done.8
  19.3 0.0 collective-permute-done.7
  19.4 2.8 %collective-permute-start.10 = (f32[256,64]{1,0:T(8,128)S(1)}, f32[256,64]{1,0:T(8,128)S(1)}, u32[]{:S(2)}, u32[]{:S(2)}) collective-permute-start(f32[256,64]{1,0:T(8,128)S(1)} %select_select_fusion.1), channel_id=1, source_target_pairs={{0,8},{8,0},{16,24},{24,16},{32,40},{40,32},{48,56},{56,48},{64,72... | collective-permute-start | bytes 196616 | tf_op jit(solution)/shard_map/ppermute | solution.py:271
  22.1 0.0 collective-permute-done.5
  22.1 0.0 collective-permute-done.4
  22.2 9.8 %collective-permute-done.3 = f32[2,256,64]{2,1,0:T(8,128)S(1)} collective-permute-done((f32[2,256,64]{2,1,0:T(8,128)S(1)}, f32[2,256,64]{2,1,0:T(8,128)S(1)}, u32[]{:S(2)}, u32[]{:S(2)}) %collective-permute-start.3) | collective-permute-done | bytes 131104 | tf_op jit(solution)/shard_map/ppermute | solution.py:253
  32.0 0.1 select_select_fusion
  32.0 3.0 %collective-permute-start.6 = (f32[2,256,64]{2,1,0:T(8,128)S(1)}, f32[2,256,64]{2,1,0:T(8,128)S(1)}, u32[]{:S(2)}, u32[]{:S(2)}) collective-permute-start(f32[2,256,64]{2,1,0:T(8,128)S(1)} %select_select_fusion), channel_id=1, source_target_pairs={{0,8},{8,0},{16,24},{24,16},{32,40},{40,32},{48,56},{56,48},{64,72... | collective-permute-start | bytes 393224 | tf_op jit(solution)/shard_map/ppermute | solution.py:282
  35.1 0.0 collective-permute-done.10
  35.1 0.0 copy-done
  35.1 21.8 %panel_factor.1 = (f32[512,512]{1,0:T(8,128)S(1)}, f32[512,512]{1,0:T(8,128)S(1)}) custom-call(f32[512,64]{1,0:T(8,128)S(1)} %maximum_select_fusion.panel_ref, f32[1,64]{1,0:T(1,128)S(1)} %bitcast.11), custom_call_target="tpu_custom_call" | custom-call | tf_op jit(solution)/shard_map/panel_factor/pallas_call | solution.py:152
  57.0 0.0 collective-permute-done.6
  57.1 15.1 %trailing_update.1 = (f32[512,2048]{1,0:T(8,128)}, f32[512,512]{1,0:T(8,128)S(1)}) custom-call(f32[256,64]{1,0:T(8,128)S(1)} %copy.22.own_ref, f32[1024,64]{1,0:T(8,128)S(1)} %bitcast.10, f32[512,64]{1,0:T(8,128)S(1)} %maximum_select_fusion.panel_ref, f32[1,64]{1,0:T(1,128)S(1)} %bitcast.12, f32[512,512]{1,0:T(8,128)S(1)} %get-tuple-element.7.inverse_ref, ...), custom_call_target="tpu_custom_call" | custom-call | tf_op jit(solution)/shard_map/trailing_update/pallas_call | solution.py:216
  72.2 0.2 constant_dynamic-slice_fusion
  72.4 0.8 %copy.25 = f32[512,64]{0,1:T(8,128)} copy(f32[512,64]{1,0:T(8,128)S(1)} %get-tuple-element.22) | data formatting | bytes 262144
  73.2 0.8 %copy.24 = f32[512,64]{0,1:T(8,128)} copy(f32[512,64]{1,0:T(8,128)S(1)} %get-tuple-element.23) | data formatting | bytes 262144
  (6 shorter events, 0.2 us)
Async XLA Ops:
  0.6 34.5 %copy-start = (f32[64]{0:T(128)S(1)}, f32[64]{0:T(128)}, u32[]{:S(2)}) copy-start(f32[64]{0:T(128)} %param.4) | copy-start | bytes 772
  1.6 5.7 %collective-permute-start.2 = (f32[256,64]{1,0:T(8,128)S(1)}, f32[256,64]{1,0:T(8,128)S(1)}, u32[]{:S(2)}, u32[]{:S(2)}) collective-permute-start(f32[256,64]{1,0:T(8,128)S(1)} %copy.22.own_ref), channel_id=1, source_target_pairs={{0,16},{8,24},{16,32},{24,40},{32,48},{40,56},{48,0},{56,8},{64,80... | collective-permute-start | bytes 196616 | tf_op jit(solution)/shard_map/ppermute | solution.py:256
  2.9 8.2 %collective-permute-start.1 = (f32[256,64]{1,0:T(8,128)S(1)}, f32[256,64]{1,0:T(8,128)S(1)}, u32[]{:S(2)}, u32[]{:S(2)}) collective-permute-start(f32[256,64]{1,0:T(8,128)S(1)} %copy.22.own_ref), channel_id=1, source_target_pairs={{0,32},{8,40},{16,48},{24,56},{32,0},{40,8},{48,16},{56,24},{64,96... | collective-permute-start | bytes 196616 | tf_op jit(solution)/shard_map/ppermute | solution.py:256
  5.3 5.7 %collective-permute-start = (f32[256,64]{1,0:T(8,128)S(1)}, f32[256,64]{1,0:T(8,128)S(1)}, u32[]{:S(2)}, u32[]{:S(2)}) collective-permute-start(f32[256,64]{1,0:T(8,128)S(1)} %copy.22.own_ref), channel_id=1, source_target_pairs={{0,48},{8,56},{16,0},{24,8},{32,16},{40,24},{48,32},{56,40},{64,11... | collective-permute-start | bytes 196616 | tf_op jit(solution)/shard_map/ppermute | solution.py:256
  11.1 6.9 %collective-permute-start.9 = (f32[256,64]{1,0:T(8,128)S(1)}, f32[256,64]{1,0:T(8,128)S(1)}, u32[]{:S(2)}, u32[]{:S(2)}) collective-permute-start(f32[256,64]{1,0:T(8,128)S(1)} %get-tuple-element.17), channel_id=1, source_target_pairs={{192,0},{200,8},{208,16},{216,24},{224,32},{232,40},{240,48},{248,... | collective-permute-start | bytes 196616 | tf_op jit(solution)/shard_map/ppermute | solution.py:253
  12.4 6.9 %collective-permute-start.8 = (f32[256,64]{1,0:T(8,128)S(1)}, f32[256,64]{1,0:T(8,128)S(1)}, u32[]{:S(2)}, u32[]{:S(2)}) collective-permute-start(f32[256,64]{1,0:T(8,128)S(1)} %get-tuple-element.17), channel_id=1, source_target_pairs={{192,64},{200,72},{208,80},{216,88},{224,96},{232,104},{240,112},{... | collective-permute-start | bytes 196616 | tf_op jit(solution)/shard_map/ppermute | solution.py:253
  13.1 6.2 %collective-permute-start.7 = (f32[256,64]{1,0:T(8,128)S(1)}, f32[256,64]{1,0:T(8,128)S(1)}, u32[]{:S(2)}, u32[]{:S(2)}) collective-permute-start(f32[256,64]{1,0:T(8,128)S(1)} %get-tuple-element.17), channel_id=1, source_target_pairs={{192,128},{200,136},{208,144},{216,152},{224,160},{232,168},{240,1... | collective-permute-start | bytes 196616 | tf_op jit(solution)/shard_map/ppermute | solution.py:253
  13.8 8.4 %collective-permute-start.5 = (f32[2,256,64]{2,1,0:T(8,128)S(1)}, f32[2,256,64]{2,1,0:T(8,128)S(1)}, u32[]{:S(2)}, u32[]{:S(2)}) collective-permute-start(f32[2,256,64]{2,1,0:T(8,128)S(1)} %pad_maximum_fusion.1), channel_id=1, source_target_pairs={{0,64},{8,72},{16,80},{24,88},{32,96},{40,104},{48,112},{56,120},{... | collective-permute-start | bytes 393224 | tf_op jit(solution)/shard_map/ppermute | solution.py:253
  14.5 7.7 %collective-permute-start.4 = (f32[2,256,64]{2,1,0:T(8,128)S(1)}, f32[2,256,64]{2,1,0:T(8,128)S(1)}, u32[]{:S(2)}, u32[]{:S(2)}) collective-permute-start(f32[2,256,64]{2,1,0:T(8,128)S(1)} %pad_maximum_fusion.1), channel_id=1, source_target_pairs={{0,128},{8,136},{16,144},{24,152},{32,160},{40,168},{48,176},{56,1... | collective-permute-start | bytes 393224 | tf_op jit(solution)/shard_map/ppermute | solution.py:253
  18.0 14.0 %collective-permute-start.3 = (f32[2,256,64]{2,1,0:T(8,128)S(1)}, f32[2,256,64]{2,1,0:T(8,128)S(1)}, u32[]{:S(2)}, u32[]{:S(2)}) collective-permute-start(f32[2,256,64]{2,1,0:T(8,128)S(1)} %pad_maximum_fusion.1), channel_id=1, source_target_pairs={{0,192},{8,200},{16,208},{24,216},{32,224},{40,232},{48,240},{56,2... | collective-permute-start | bytes 393224 | tf_op jit(solution)/shard_map/ppermute | solution.py:253
  19.4 15.7 %collective-permute-start.10 = (f32[256,64]{1,0:T(8,128)S(1)}, f32[256,64]{1,0:T(8,128)S(1)}, u32[]{:S(2)}, u32[]{:S(2)}) collective-permute-start(f32[256,64]{1,0:T(8,128)S(1)} %select_select_fusion.1), channel_id=1, source_target_pairs={{0,8},{8,0},{16,24},{24,16},{32,40},{40,32},{48,56},{56,48},{64,72... | collective-permute-start | bytes 196616 | tf_op jit(solution)/shard_map/ppermute | solution.py:271
  32.0 24.9 %collective-permute-start.6 = (f32[2,256,64]{2,1,0:T(8,128)S(1)}, f32[2,256,64]{2,1,0:T(8,128)S(1)}, u32[]{:S(2)}, u32[]{:S(2)}) collective-permute-start(f32[2,256,64]{2,1,0:T(8,128)S(1)} %select_select_fusion), channel_id=1, source_target_pairs={{0,8},{8,0},{16,24},{24,16},{32,40},{40,32},{48,56},{56,48},{64,72... | collective-permute-start | bytes 393224 | tf_op jit(solution)/shard_map/ppermute | solution.py:282

commit v2 on v1

v2 whole, which is shorter than its diff:
```python
import math

import jax
import jax.numpy as jnp
from jax import lax
from jax.experimental import pallas as pl
from jax.experimental.pallas import tpu as pltpu
from jax.sharding import PartitionSpec as P

PANEL = 512
DIM = 64
BLOCK = 128
GROUP = 8

signal_variance = 4.0
nugget_level = 0.1

F32 = jnp.float32
BF16 = jnp.bfloat16
HIGHEST = lax.Precision.HIGHEST
NT = (((1,), (1,)), ((), ()))
NN = (((1,), (0,)), ((), ()))


def dot_nt(a, b):
    return lax.dot_general(a, b, NT, precision=HIGHEST, preferred_element_type=F32)


def dot_nn(a, b):
    return lax.dot_general(a, b, NN, precision=HIGHEST, preferred_element_type=F32)


def split(x):
    hi = x.astype(BF16)
    return hi, (x - hi.astype(F32)).astype(BF16)


def dot_one(a, b, dims):
    return lax.dot_general(a, b, dims, preferred_element_type=F32)


def dot_split(a, b, dims=NT):
    return dot_one(a[0], b[0], dims) + (dot_one(a[0], b[1], dims) + dot_one(a[1], b[0], dims))


def lane_take(x, lanes):
    return jnp.take_along_axis(x, lanes, axis=1, mode="promise_in_bounds")


def lane_spread(x, lane):
    return lane_take(x, jnp.full(x.shape, lane, jnp.int32))


def row_spread(x, row):
    return jnp.broadcast_to(x[row : row + 1, :], (8, 128))


def factor_block(rows):
    lane = lax.broadcasted_iota(jnp.int32, (8, 128), 1)
    sub = lax.broadcasted_iota(jnp.int32, (8, 128), 0)
    rows = list(rows)
    cols = [lane_spread(rows[0], j) for j in range(GROUP)]
    for g in range(len(rows)):
        base = GROUP * g
        slab = rows[g]
        s = [[row_spread(cols[j], k) if k <= j else None for j in range(GROUP)] for k in range(GROUP)]
        r = [None] * GROUP
        u = [[None] * GROUP for _ in range(GROUP)]
        for k in range(GROUP):
            r[k] = lax.rsqrt(s[k][k])
            for j in range(k + 1, GROUP):
                u[k][j] = s[k][j] * r[k]
            for i in range(k + 1, GROUP):
                for j in range(i, GROUP):
                    s[i][j] = s[i][j] - u[k][i] * u[k][j]
        pivots = []
        clean = []
        within = (lane >= base) & (lane < base + GROUP)
        final = slab
        for k in range(GROUP):
            row = row_spread(slab, k)
            for m in range(k):
                row = row - u[m][k] * pivots[m]
            row = row * r[k]
            diag = lane == base + k
            own = jnp.where(diag, r[k], row)
            final = jnp.where(sub == k, own, final)
            clean.append(jnp.where(within & (lane > base + k), 0.0, own))
            pivots.append(jnp.where(diag, s[k][k] * r[k] + r[k], row))
        rows[g] = final
        for i in range(g + 1, len(rows)):
            x = rows[i]
            if i == g + 1:
                c = [lane_spread(x, base + j) for j in range(GROUP)]
                cols = [lane_spread(x, base + GROUP + j) for j in range(GROUP)]
                for k in range(GROUP):
                    low = c[k] * r[k]
                    for j in range(k + 1, GROUP):
                        c[j] = c[j] - low * u[k][j]
                    cols = [cols[j] - low * row_spread(low, j) for j in range(GROUP)]
                    x = x - low * pivots[k]
            else:
                x = jnp.where(within, 0.0, x)
                for k in range(GROUP):
                    x = x - lane_take(clean[k], GROUP * i + sub) * clean[k]
            rows[i] = x
    return rows


def kernel_values(rows, points):
    squares_rows = jnp.sum(rows * rows, axis=1, keepdims=True)
    squares_points = jnp.sum(points * points, axis=0, keepdims=True)
    gaps = squares_rows + squares_points - 2.0 * dot_nn(rows, points)
    return signal_variance * jnp.exp(-gaps)


def gap_along(rows, points, d):
    return rows[:, d : d + 1] - points[d : d + 1, :]


def roots_column(roots_ref):
    return jnp.broadcast_to(roots_ref[...], (8, DIM)).T[:, 0:1]


def factor_kernel(col_ref, first_ref, second_ref, roots_ref, shard_ref, inverse_ref, factor_ref, work_ref, block_ref, turn_ref):
    points = jnp.concatenate([first_ref[...], second_ref[...]], 1) * roots_column(roots_ref)
    rows = points.T
    kernel = kernel_values(rows, points)
    gap = gap_along(rows, points, DIM - 2)
    row_iota = lax.broadcasted_iota(jnp.int32, (PANEL, PANEL), 0)
    col_iota = lax.broadcasted_iota(jnp.int32, (PANEL, PANEL), 1)
    work_ref[...] = kernel * (1.0 - 2.0 * gap * gap) + jnp.where(row_iota == col_iota, nugget_level, 0.0)
    factor_ref[...] = jnp.zeros_like(factor_ref)
    inverse_ref[...] = jnp.zeros_like(inverse_ref)

    @pl.loop(0, PANEL // BLOCK)
    def _(step):
        at = pl.multiple_of(step * BLOCK, BLOCK)
        rows = [work_ref[pl.ds(at + 8 * i, 8), pl.ds(at, BLOCK)] for i in range(BLOCK // 8)]
        rows = factor_block(rows)
        for i in range(BLOCK // 8):
            block_ref[8 * i : 8 * i + 8, :] = rows[i]
        both = block_ref[...]
        r = lax.broadcasted_iota(jnp.int32, (BLOCK, BLOCK), 0)
        c = lax.broadcasted_iota(jnp.int32, (BLOCK, BLOCK), 1)
        upper = jnp.where(c > r, both, jnp.where(c == r, 1.0 / both, 0.0))
        factor_ref[pl.ds(at, BLOCK), pl.ds(at, BLOCK)] = upper.T
        inverse = jnp.where(c <= r, both, 0.0)
        inverse_ref[pl.ds(at, BLOCK), pl.ds(at, BLOCK)] = inverse
        for s in range(PANEL // BLOCK - 1):

            @pl.when(step == s)
            def _():
                end = BLOCK * (s + 1)
                below = dot_nt(work_ref[end:, end - BLOCK : end], inverse)
                factor_ref[end:, end - BLOCK : end] = below
                work_ref[end:, end:] = work_ref[end:, end:] - dot_nt(below, below)

    for n in (BLOCK, 2 * BLOCK):
        for t in range(0, PANEL, 2 * n):
            left = dot_nn(factor_ref[t + n : t + 2 * n, t : t + n], inverse_ref[t : t + n, t : t + n])
            inverse_ref[t + n : t + 2 * n, t : t + n] = -dot_nn(
                inverse_ref[t + n : t + 2 * n, t + n : t + 2 * n], left
            )

    width = shard_ref.shape[0]
    start = col_ref[0] * width
    for s in range(PANEL // BLOCK):

        @pl.when(start // BLOCK == s)
        def _():
            turn_ref[...] = factor_ref[:, BLOCK * s : BLOCK * s + BLOCK].T
            shard_ref[...] = turn_ref[pl.ds(pl.multiple_of(start - BLOCK * s, width), width), :]


IN_SMEM = pl.BlockSpec(memory_space=pltpu.SMEM)
IN_VMEM = pl.BlockSpec(memory_space=pltpu.VMEM)


def factor_call(col, width, first, second, roots):
    return pl.pallas_call(
        factor_kernel,
        in_specs=[IN_SMEM, IN_VMEM, IN_VMEM, IN_VMEM],
        out_shape=[jax.ShapeDtypeStruct((width, PANEL), F32), jax.ShapeDtypeStruct((PANEL, PANEL), F32)],
        scratch_shapes=[
            pltpu.VMEM((PANEL, PANEL), F32), pltpu.VMEM((PANEL, PANEL), F32), pltpu.VMEM((BLOCK, BLOCK), F32),
            pltpu.VMEM((BLOCK, PANEL), F32),
        ],
        compiler_params=pltpu.CompilerParams(vmem_limit_bytes=32 << 20),
        name="panel_factor",
    )(col, first, second, roots)


def cross_rows(designs, root_weights, points, cross_ref):
    rows = (designs * root_weights).T
    kernel = kernel_values(rows, points)
    gap_u = gap_along(rows, points, DIM - 2)
    gap_v = gap_along(rows, points, DIM - 1)
    n = rows.shape[0]
    derivative = -2.0 * kernel * gap_v * gap_u
    value = math.sqrt(2.0) * kernel * gap_u
    for q in range(PANEL // 128):
        cross_ref[q, pl.ds(0, n, stride=2), :] = derivative[:, 128 * q : 128 * q + 128]
        cross_ref[q, pl.ds(1, n, stride=2), :] = value[:, 128 * q : 128 * q + 128]
    return jnp.concatenate([cross_ref[q] for q in range(PANEL // 128)], 1)


def update_kernel(
    col_ref, own_ref, first_ref, second_ref, roots_ref, inverse_ref, far_ref, trailing_ref,
    updated_ref, shard_ref, points_ref, root_ref, hi_ref, lo_ref, cross_ref, tiles_ref, sems,
):
    half = PANEL // 2
    step = pl.program_id(0)
    steps, _, tile_width = tiles_ref.shape

    def tile_copy(j):
        columns = trailing_ref.at[:, pl.ds(pl.multiple_of(j * tile_width, 128), tile_width)]
        return pltpu.make_async_copy(columns, tiles_ref.at[j], sems.at[j])

    @pl.when(step == 0)
    def _():
        for j in range(steps):
            tile_copy(j).start()
        root_ref[...] = roots_column(roots_ref)
        points_ref[...] = jnp.concatenate([first_ref[...], second_ref[...]], 1) * root_ref[...]
        cross = cross_rows(own_ref[...], root_ref[...], points_ref[...], cross_ref)
        left = dot_nt(cross[:, :half], inverse_ref[:half, :half])
        right = dot_nt(cross, inverse_ref[half:, :])
        left_hi, left_lo = split(left)
        right_hi, right_lo = split(right)
        rows_hi = jnp.concatenate([left_hi, right_hi], 1)
        rows_lo = jnp.concatenate([left_lo, right_lo], 1)
        width = shard_ref.shape[0]
        chosen = lax.broadcasted_iota(jnp.int32, (width, PANEL), 0) + col_ref[0] * width
        pick = jnp.where(lax.broadcasted_iota(jnp.int32, (width, PANEL), 1) == chosen, 1.0, 0.0).astype(BF16)
        shard_ref[...] = dot_one(pick, rows_hi, NT) + dot_one(pick, rows_lo, NT)
        inv_hi, inv_lo = split(inverse_ref[...])
        left = dot_split((rows_hi, rows_lo), (inv_hi[:, :half], inv_lo[:, :half]), NN)
        right = dot_split((right_hi, right_lo), (inv_hi[half:, half:], inv_lo[half:, half:]), NN)
        hi_ref[:, :half], lo_ref[:, :half] = split(left)
        hi_ref[:, half:], lo_ref[:, half:] = split(right)

    far = split(cross_rows(far_ref[0], root_ref[...], points_ref[...], cross_ref))
    product = dot_split((hi_ref[...], lo_ref[...]), far)
    tile_copy(step).wait()
    updated_ref[...] = tiles_ref[step] - product


def update_call(col, panel_width, own, first, second, roots, inverse, far, trailing):
    n = own.shape[1]
    height, width = trailing.shape
    steps = far.shape[0]
    tile = pl.BlockSpec((height, width // steps), lambda j: (0, j))
    return pl.pallas_call(
        update_kernel,
        grid=(steps,),
        in_specs=[
            IN_SMEM, IN_VMEM, IN_VMEM, IN_VMEM, IN_VMEM, IN_VMEM, pl.BlockSpec((1, DIM, n), lambda j: (j, 0, 0)),
            pl.BlockSpec(memory_space=pltpu.HBM),
        ],
        out_specs=[tile, pl.BlockSpec((panel_width, height), lambda j: (0, 0))],
        out_shape=[jax.ShapeDtypeStruct((height, width), F32), jax.ShapeDtypeStruct((panel_width, height), F32)],
        scratch_shapes=[
            pltpu.VMEM((DIM, PANEL), F32), pltpu.VMEM((DIM, 1), F32), pltpu.VMEM((height, PANEL), BF16),
            pltpu.VMEM((height, PANEL), BF16), pltpu.VMEM((PANEL // 128, 2 * n, 128), F32),
            pltpu.VMEM((steps, height, width // steps), F32), pltpu.SemaphoreType.DMA((steps,)),
        ],
        compiler_params=pltpu.CompilerParams(vmem_limit_bytes=48 << 20, dimension_semantics=("arbitrary",)),
        name="trailing_update",
    )(col, own, first, second, roots, inverse, far, pltpu.with_memory_space_constraint(trailing, pltpu.HBM))


NY, NX, NC = 4, 4, 2
DEVICES = NY * NX * NC


def place(y, x, core):
    return (y * NX + x) * NC + core


def gather_designs(designs, roots):
    at = lax.axis_index("prow")
    col = lax.axis_index("pcol")
    x_at, y_at, core = at // NC % NX, at // (NX * NC), at % NC
    cores, xs, ys = range(NC), range(NX), range(NY)
    along_x = [[(place(y, x, c), place(y, (x + s) % NX, c)) for y in ys for x in xs for c in cores] for s in range(NX)]
    along_y = [[(place(y, x, c), place((y + s) % NY, x, c)) for y in ys for x in xs for c in cores] for s in range(NY)]
    swap = [(j, j ^ 1) for j in range(DEVICES)]
    send = lambda block, pairs: lax.ppermute(block, "prow", pairs)

    def rounds(block, pairs):
        got = {s: send(block, pairs[s]) for s in (2, 1, 3)}
        return [block] + [got[s] for s in (1, 2, 3)]

    def pick(blocks, shift):
        chosen = blocks[0]
        for s in range(1, len(blocks)):
            chosen = jnp.where(shift == s, blocks[s], chosen)
        return chosen

    from_x = rounds(designs, along_x)
    block_of = lambda x: pick(from_x, (x_at - x) % NX)
    panel, roots = lax.optimization_barrier((block_of(NX - 1), roots))
    panel = pick(rounds(panel, along_y), (y_at - (NY - 1)) % NY)
    half = 2 * (col % 2)
    far = jnp.stack([block_of(half), block_of(half + 1)], 0)
    far_other = send(far, swap)
    other = send(panel, swap)
    first = jnp.where(core == 0, panel, other)
    second = jnp.where(core == 0, other, panel)
    far = jnp.stack([jnp.where(core == 0, far, far_other), jnp.where(core == 0, far_other, far)], 1)
    far = far.reshape(2 * NC, *designs.shape)
    first, second, far = lax.optimization_barrier((first, second, far))
    far = pick(rounds(far, along_y), (y_at - col // 2) % NY)
    return first, second, far, roots


def body(designs, length_weights, trailing):
    width = PANEL // lax.axis_size("pcol")
    col = lax.axis_index("pcol").reshape(1)
    own = designs.T
    first, second, far, roots = gather_designs(own, jnp.sqrt(length_weights).reshape(1, DIM))
    factor_shard, inverse = factor_call(col, width, first, second, roots)
    updated, rows_shard = update_call(col, width, own, first, second, roots, inverse, far, trailing)
    return updated, rows_shard.T, factor_shard.T


def solution(mesh):
    in_specs = (P("prow", None), P(), P("prow", "pcol"))
    out_specs = (P("prow", "pcol"), P("prow", "pcol"), P(None, "pcol"))
    return jax.shard_map(body, mesh=mesh, in_specs=in_specs, out_specs=out_specs, check_vma=False)
```

time: 74.2 us -> 55.2 us (0.74)
  waiting for transfers between devices: 17.3 us -> 2.89 us
  Pallas kernels: 36.9 us -> 29.6 us
  starting transfers between devices: 16 us -> 19.2 us
  local copies, waits for them, and re-layouts: 2.72 us -> 0.68 us
  other arithmetic: 0.26 us -> 1.02 us
    ppermute x11, waiting for transfers between devices: 17.3 us -> 2.89 us  [gather_designs(): send = lambda block, pairs: lax.ppermute(block, 'prow', pairs)]
    pallas_call x2, Pallas kernels: 36.9 us -> 29.6 us  [the longest x1 16.6 us: factor_call(): pl.pallas_call(factor_kernel, in_specs=[IN_SMEM, IN_VMEM, IN_VMEM, IN_VME...]
    ppermute x11, starting transfers between devices: 16 us -> 19.2 us  [gather_designs(): send = lambda block, pairs: lax.ppermute(block, 'prow', pairs)]
    unnamed x5 -> x2, local copies, waits for them, and re-layouts: 2.49 us -> 0.01 us
    another operation x1 -> x2, other arithmetic: 0.02 us -> 0.88 us  [gather_designs(): far = jnp.stack([block_of(half), block_of(half + 1)], 0)]
  transfers between devices with their start and end apart: 11 -> 11, of which waited for: 4 -> 3; matrix products, arithmetic and copies ran while one was open for 0% -> 1% of each run, Pallas kernels for 30% -> 31%
where the time goes in v2:
time: 55.2 us; the launch traced here: 54.2 us
  Pallas kernels  29.6 us (54%)
  starting transfers between devices  19.2 us (35%)
  waiting for transfers between devices  2.89 us (5%)
  other arithmetic  1.02 us (2%)
  between operations  0.87 us (2%)
  local copies, waits for them, and re-layouts  0.68 us (1%)
    ppermute x11, starting transfers between devices, gather_designs(): send = lambda block, pairs: lax.ppermute(block, 'prow', pairs)  19.2 us
    pallas_call x1, Pallas kernels, factor_call(): pl.pallas_call(factor_kernel, in_specs=[IN_SMEM, IN_VMEM, IN_VMEM, IN_VME...  16.6 us
    pallas_call x1, Pallas kernels, update_call(): pl.pallas_call(update_kernel, grid=(steps,), in_specs=[IN_SMEM, IN_VMEM,...  13 us
    ppermute x11, waiting for transfers between devices, gather_designs(): send = lambda block, pairs: lax.ppermute(block, 'prow', pairs)  2.89 us
  transfers between devices with their start and end apart: 11, of which 3 were waited for; matrix products, arithmetic and copies ran while one was open for 1% of the time, Pallas kernels for 31%

profile of v2, /device:TPU:65, one launch (start us, length us, event | category | flops | bytes accessed | tf_op | source)
XLA Modules:
  0.0 54.2 jit_solution(10937538024565891787)
XLA Ops:
  0.6 0.0 copy-start
  0.6 1.3 %collective-permute-start.2 = (f32[64,256]{1,0:T(8,128)}, f32[64,256]{1,0:T(8,128)S(1)}, u32[]{:S(2)}, u32[]{:S(2)}) collective-permute-start(f32[64,256]{1,0:T(8,128)} %bitcast.18), channel_id=1, source_target_pairs={{0,16},{8,24},{16,32},{24,40},{32,48},{40,56},{48,0},{56,8},{64,80... | collective-permute-start | bytes 196616 | tf_op jit(solution)/shard_map/ppermute | solution.py:289
  1.9 2.5 %collective-permute-start.1 = (f32[64,256]{1,0:T(8,128)}, f32[64,256]{1,0:T(8,128)S(1)}, u32[]{:S(2)}, u32[]{:S(2)}) collective-permute-start(f32[64,256]{1,0:T(8,128)} %bitcast.19), channel_id=1, source_target_pairs={{0,32},{8,40},{16,48},{24,56},{32,0},{40,8},{48,16},{56,24},{64,96... | collective-permute-start | bytes 196616 | tf_op jit(solution)/shard_map/ppermute | solution.py:289
  4.4 1.2 %collective-permute-start = (f32[64,256]{1,0:T(8,128)}, f32[64,256]{1,0:T(8,128)S(1)}, u32[]{:S(2)}, u32[]{:S(2)}) collective-permute-start(f32[64,256]{1,0:T(8,128)} %bitcast.20), channel_id=1, source_target_pairs={{0,48},{8,56},{16,0},{24,8},{32,16},{40,24},{48,32},{56,40},{64,11... | collective-permute-start | bytes 196616 | tf_op jit(solution)/shard_map/ppermute | solution.py:289
  5.5 0.7 %sqrt_bitcast_fusion.roots_ref = f32[1,64]{1,0:T(1,128)S(1)} fusion(f32[64]{0:T(128)} %param.4), kind=kLoop, calls=%fused_computation.11 | loop fusion | bytes 512 | tf_op jit(solution)/shard_map/reshape | solution.py:322
  6.2 0.0 collective-permute-done.2
  6.2 1.0 %collective-permute-done.1 = f32[64,256]{1,0:T(8,128)S(1)} collective-permute-done((f32[64,256]{1,0:T(8,128)}, f32[64,256]{1,0:T(8,128)S(1)}, u32[]{:S(2)}, u32[]{:S(2)}) %collective-permute-start.1) | collective-permute-done | bytes 65568 | tf_op jit(solution)/shard_map/ppermute | solution.py:289
  7.2 1.1 %collective-permute-done = f32[64,256]{1,0:T(8,128)S(1)} collective-permute-done((f32[64,256]{1,0:T(8,128)}, f32[64,256]{1,0:T(8,128)S(1)}, u32[]{:S(2)}, u32[]{:S(2)}) %collective-permute-start) | collective-permute-done | bytes 65568 | tf_op jit(solution)/shard_map/ppermute | solution.py:289
  8.2 0.9 %select_bitcast_fusion.3 = (f32[1,64,256]{2,1,0:T(8,128)S(1)}, f32[1,64,256]{2,1,0:T(8,128)S(1)}, f32[64,256]{1,0:T(8,128)S(1)}) fusion(f32[64,256]{1,0:T(8,128)S(1)} %collective-permute-done, f32[64,256]{1,0:T(8,128)S(1)} %collective-permute-done.1, f32[64,256]{1,0:T(8,128)S(1)} %collective-permute-done.2, pred[]{:T(512)S(6)} %eq.69, pred[]{:T(512)S(6)} %eq.68, ...), kind=kLoop, calls=%fused_computation.6 | loop fusion | flops 147456 | bytes 458761 | tf_op jit(solution)/shard_map/stack | solution.py:306
  9.1 1.4 %collective-permute-start.5 = (f32[64,256]{1,0:T(8,128)S(1)}, f32[64,256]{1,0:T(8,128)S(1)}, u32[]{:S(2)}, u32[]{:S(2)}) collective-permute-start(f32[64,256]{1,0:T(8,128)S(1)} %get-tuple-element.12), channel_id=1, source_target_pairs={{0,64},{8,72},{16,80},{24,88},{32,96},{40,104},{48,112},{56,120},{... | collective-permute-start | bytes 196616 | tf_op jit(solution)/shard_map/ppermute | solution.py:289
  10.5 2.6 %collective-permute-start.4 = (f32[64,256]{1,0:T(8,128)S(1)}, f32[64,256]{1,0:T(8,128)S(1)}, u32[]{:S(2)}, u32[]{:S(2)}) collective-permute-start(f32[64,256]{1,0:T(8,128)S(1)} %get-tuple-element.12), channel_id=1, source_target_pairs={{0,128},{8,136},{16,144},{24,152},{32,160},{40,168},{48,176},{56,1... | collective-permute-start | bytes 196616 | tf_op jit(solution)/shard_map/ppermute | solution.py:289
  13.1 1.1 %collective-permute-start.3 = (f32[64,256]{1,0:T(8,128)S(1)}, f32[64,256]{1,0:T(8,128)S(1)}, u32[]{:S(2)}, u32[]{:S(2)}) collective-permute-start(f32[64,256]{1,0:T(8,128)S(1)} %get-tuple-element.12), channel_id=1, source_target_pairs={{0,192},{8,200},{16,208},{24,216},{32,224},{40,232},{48,240},{56,2... | collective-permute-start | bytes 196616 | tf_op jit(solution)/shard_map/ppermute | solution.py:289
  14.2 2.8 %collective-permute-start.7 = (f32[2,64,256]{2,1,0:T(8,128)S(1)}, f32[2,64,256]{2,1,0:T(8,128)S(1)}, u32[]{:S(2)}, u32[]{:S(2)}) collective-permute-start(f32[2,64,256]{2,1,0:T(8,128)S(1)} %pad_maximum_fusion.1), channel_id=1, source_target_pairs={{0,8},{8,0},{16,24},{24,16},{32,40},{40,32},{48,56},{56,48},{64,72... | collective-permute-start | bytes 393224 | tf_op jit(solution)/shard_map/ppermute | solution.py:289
  17.0 0.0 collective-permute-done.5
  17.0 0.0 collective-permute-done.4
  17.0 0.0 collective-permute-done.3
  17.0 2.9 %collective-permute-start.6 = (f32[64,256]{1,0:T(8,128)S(1)}, f32[64,256]{1,0:T(8,128)S(1)}, u32[]{:S(2)}, u32[]{:S(2)}) collective-permute-start(f32[64,256]{1,0:T(8,128)S(1)} %select_select_fusion.1), channel_id=1, source_target_pairs={{0,8},{8,0},{16,24},{24,16},{32,40},{40,32},{48,56},{56,48},{64,72... | collective-permute-start | bytes 196616 | tf_op jit(solution)/shard_map/ppermute | solution.py:289
  19.9 0.0 collective-permute-done.7
  20.0 0.8 %collective-permute-done.6 = f32[64,256]{1,0:T(8,128)S(1)} collective-permute-done((f32[64,256]{1,0:T(8,128)S(1)}, f32[64,256]{1,0:T(8,128)S(1)}, u32[]{:S(2)}, u32[]{:S(2)}) %collective-permute-start.6) | collective-permute-done | bytes 65568 | tf_op jit(solution)/shard_map/ppermute | solution.py:289
  20.8 0.1 collective-permute-start.10
  20.9 3.4 %collective-permute-start.9 = (f32[4,64,256]{2,1,0:T(8,128)S(1)}, f32[4,64,256]{2,1,0:T(8,128)S(1)}, u32[]{:S(2)}, u32[]{:S(2)}) collective-permute-start(f32[4,64,256]{2,1,0:T(8,128)S(1)} %bitcast.23), channel_id=1, source_target_pairs={{0,128},{8,136},{16,144},{24,152},{32,160},{40,168},{48,176},{56,1... | collective-permute-start | bytes 786440 | tf_op jit(solution)/shard_map/ppermute | solution.py:289
  24.3 0.0 collective-permute-start.8
  24.4 16.6 %panel_factor.1 = (f32[64,512]{1,0:T(8,128)}, f32[512,512]{1,0:T(8,128)S(1)}) custom-call(s32[1]{0:T(128)} %bitcast.col_ref, f32[64,256]{1,0:T(8,128)S(1)} %get-tuple-element.13.first_ref, f32[64,256]{1,0:T(8,128)S(1)} %get-tuple-element.14.second_ref, f32[1,64]{1,0:T(1,128)S(1)} %sqrt_bitcast_fusion.roots_ref), custom_call_target="tpu_custom_call" | custom-call | tf_op jit(solution)/shard_map/panel_factor/pallas_call | solution.py:181
  41.0 0.0 collective-permute-done.10
  41.0 0.0 collective-permute-done.9
  41.0 0.0 collective-permute-done.8
  41.0 0.1 select_select_fusion.far_ref
  41.0 0.0 copy-done
  41.1 13.0 %trailing_update.1 = (f32[512,2048]{1,0:T(8,128)}, f32[64,512]{1,0:T(8,128)}) custom-call(s32[1]{0:T(128)} %bitcast.col_ref, f32[64,256]{1,0:T(8,128)S(1)} %bitcast.21, f32[64,256]{1,0:T(8,128)S(1)} %get-tuple-element.13.first_ref, f32[64,256]{1,0:T(8,128)S(1)} %get-tuple-element.14.second_ref, f32[1,64]{1,0:T(1,128)S(1)} %sqrt_bitcast_fusion.roots_ref, ...), custom_call_target="tpu_custom_call" | custom-call | tf_op jit(solution)/shard_map/trailing_update/pallas_call | solution.py:254
  (6 shorter events, 0.1 us)
Async XLA Ops:
  0.6 40.4 %copy-start = (f32[256,64]{0,1:T(8,128)S(1)}, f32[256,64]{0,1:T(8,128)}, u32[]{:S(2)}) copy-start(f32[256,64]{0,1:T(8,128)} %param.3) | copy-start | bytes 196612
  0.6 5.6 %collective-permute-start.2 = (f32[64,256]{1,0:T(8,128)}, f32[64,256]{1,0:T(8,128)S(1)}, u32[]{:S(2)}, u32[]{:S(2)}) collective-permute-start(f32[64,256]{1,0:T(8,128)} %bitcast.18), channel_id=1, source_target_pairs={{0,16},{8,24},{16,32},{24,40},{32,48},{40,56},{48,0},{56,8},{64,80... | collective-permute-start | bytes 196616 | tf_op jit(solution)/shard_map/ppermute | solution.py:289
  1.9 5.3 %collective-permute-start.1 = (f32[64,256]{1,0:T(8,128)}, f32[64,256]{1,0:T(8,128)S(1)}, u32[]{:S(2)}, u32[]{:S(2)}) collective-permute-start(f32[64,256]{1,0:T(8,128)} %bitcast.19), channel_id=1, source_target_pairs={{0,32},{8,40},{16,48},{24,56},{32,0},{40,8},{48,16},{56,24},{64,96... | collective-permute-start | bytes 196616 | tf_op jit(solution)/shard_map/ppermute | solution.py:289
  4.4 3.9 %collective-permute-start = (f32[64,256]{1,0:T(8,128)}, f32[64,256]{1,0:T(8,128)S(1)}, u32[]{:S(2)}, u32[]{:S(2)}) collective-permute-start(f32[64,256]{1,0:T(8,128)} %bitcast.20), channel_id=1, source_target_pairs={{0,48},{8,56},{16,0},{24,8},{32,16},{40,24},{48,32},{56,40},{64,11... | collective-permute-start | bytes 196616 | tf_op jit(solution)/shard_map/ppermute | solution.py:289
  9.1 7.9 %collective-permute-start.5 = (f32[64,256]{1,0:T(8,128)S(1)}, f32[64,256]{1,0:T(8,128)S(1)}, u32[]{:S(2)}, u32[]{:S(2)}) collective-permute-start(f32[64,256]{1,0:T(8,128)S(1)} %get-tuple-element.12), channel_id=1, source_target_pairs={{0,64},{8,72},{16,80},{24,88},{32,96},{40,104},{48,112},{56,120},{... | collective-permute-start | bytes 196616 | tf_op jit(solution)/shard_map/ppermute | solution.py:289
  10.5 6.5 %collective-permute-start.4 = (f32[64,256]{1,0:T(8,128)S(1)}, f32[64,256]{1,0:T(8,128)S(1)}, u32[]{:S(2)}, u32[]{:S(2)}) collective-permute-start(f32[64,256]{1,0:T(8,128)S(1)} %get-tuple-element.12), channel_id=1, source_target_pairs={{0,128},{8,136},{16,144},{24,152},{32,160},{40,168},{48,176},{56,1... | collective-permute-start | bytes 196616 | tf_op jit(solution)/shard_map/ppermute | solution.py:289
  13.1 3.9 %collective-permute-start.3 = (f32[64,256]{1,0:T(8,128)S(1)}, f32[64,256]{1,0:T(8,128)S(1)}, u32[]{:S(2)}, u32[]{:S(2)}) collective-permute-start(f32[64,256]{1,0:T(8,128)S(1)} %get-tuple-element.12), channel_id=1, source_target_pairs={{0,192},{8,200},{16,208},{24,216},{32,224},{40,232},{48,240},{56,2... | collective-permute-start | bytes 196616 | tf_op jit(solution)/shard_map/ppermute | solution.py:289
  14.2 5.7 %collective-permute-start.7 = (f32[2,64,256]{2,1,0:T(8,128)S(1)}, f32[2,64,256]{2,1,0:T(8,128)S(1)}, u32[]{:S(2)}, u32[]{:S(2)}) collective-permute-start(f32[2,64,256]{2,1,0:T(8,128)S(1)} %pad_maximum_fusion.1), channel_id=1, source_target_pairs={{0,8},{8,0},{16,24},{24,16},{32,40},{40,32},{48,56},{56,48},{64,72... | collective-permute-start | bytes 393224 | tf_op jit(solution)/shard_map/ppermute | solution.py:289
  17.0 3.8 %collective-permute-start.6 = (f32[64,256]{1,0:T(8,128)S(1)}, f32[64,256]{1,0:T(8,128)S(1)}, u32[]{:S(2)}, u32[]{:S(2)}) collective-permute-start(f32[64,256]{1,0:T(8,128)S(1)} %select_select_fusion.1), channel_id=1, source_target_pairs={{0,8},{8,0},{16,24},{24,16},{32,40},{40,32},{48,56},{56,48},{64,72... | collective-permute-start | bytes 196616 | tf_op jit(solution)/shard_map/ppermute | solution.py:289
  20.8 20.1 %collective-permute-start.10 = (f32[4,64,256]{2,1,0:T(8,128)S(1)}, f32[4,64,256]{2,1,0:T(8,128)S(1)}, u32[]{:S(2)}, u32[]{:S(2)}) collective-permute-start(f32[4,64,256]{2,1,0:T(8,128)S(1)} %bitcast.22), channel_id=1, source_target_pairs={{0,64},{8,72},{16,80},{24,88},{32,96},{40,104},{48,112},{56,120},{... | collective-permute-start | bytes 786440 | tf_op jit(solution)/shard_map/ppermute | solution.py:289
  20.9 20.0 %collective-permute-start.9 = (f32[4,64,256]{2,1,0:T(8,128)S(1)}, f32[4,64,256]{2,1,0:T(8,128)S(1)}, u32[]{:S(2)}, u32[]{:S(2)}) collective-permute-start(f32[4,64,256]{2,1,0:T(8,128)S(1)} %bitcast.23), channel_id=1, source_target_pairs={{0,128},{8,136},{16,144},{24,152},{32,160},{40,168},{48,176},{56,1... | collective-permute-start | bytes 786440 | tf_op jit(solution)/shard_map/ppermute | solution.py:289
  24.3 16.6 %collective-permute-start.8 = (f32[4,64,256]{2,1,0:T(8,128)S(1)}, f32[4,64,256]{2,1,0:T(8,128)S(1)}, u32[]{:S(2)}, u32[]{:S(2)}) collective-permute-start(f32[4,64,256]{2,1,0:T(8,128)S(1)} %bitcast.24), channel_id=1, source_target_pairs={{0,192},{8,200},{16,208},{24,216},{32,224},{40,232},{48,240},{56,2... | collective-permute-start | bytes 786440 | tf_op jit(solution)/shard_map/ppermute | solution.py:289

commit v3 on v2

--- a/solution.py
+++ b/solution.py
@@ -20,6 +20,7 @@
 HIGHEST = lax.Precision.HIGHEST
 NT = (((1,), (1,)), ((), ()))
 NN = (((1,), (0,)), ((), ()))
+TN = (((0,), (0,)), ((), ()))
 
 
 def dot_nt(a, b):
@@ -107,11 +108,29 @@
     return rows
 
 
-def kernel_values(rows, points):
+def thirds(x):
+    first = x.astype(BF16)
+    rest = x - first.astype(F32)
+    second = rest.astype(BF16)
+    return first, second, (rest - second.astype(F32)).astype(BF16)
+
+
+def stack_left(x):
+    a, b, c = thirds(x)
+    return jnp.concatenate([a, a, b, b, a, c], 0)
+
+
+def stack_right(x):
+    a, b, c = thirds(x)
+    return jnp.concatenate([a, b, a, b, c, a], 0)
+
+
+def kernel_values(scaled, points, stacked_points):
+    rows = scaled.T
     squares_rows = jnp.sum(rows * rows, axis=1, keepdims=True)
     squares_points = jnp.sum(points * points, axis=0, keepdims=True)
-    gaps = squares_rows + squares_points - 2.0 * dot_nn(rows, points)
-    return signal_variance * jnp.exp(-gaps)
+    inner = dot_one(stack_left(scaled), stacked_points, TN)
+    return rows, signal_variance * jnp.exp(-(squares_rows + squares_points - 2.0 * inner))
 
 
 def gap_along(rows, points, d):
@@ -124,8 +143,7 @@
 
 def factor_kernel(col_ref, first_ref, second_ref, roots_ref, shard_ref, inverse_ref, factor_ref, work_ref, block_ref, turn_ref):
     points = jnp.concatenate([first_ref[...], second_ref[...]], 1) * roots_column(roots_ref)
-    rows = points.T
-    kernel = kernel_values(rows, points)
+    rows, kernel = kernel_values(points, points, stack_right(points))
     gap = gap_along(rows, points, DIM - 2)
     row_iota = lax.broadcasted_iota(jnp.int32, (PANEL, PANEL), 0)
     col_iota = lax.broadcasted_iota(jnp.int32, (PANEL, PANEL), 1)
@@ -191,9 +209,8 @@
     )(col, first, second, roots)
 
 
-def cross_rows(designs, root_weights, points, cross_ref):
-    rows = (designs * root_weights).T
-    kernel = kernel_values(rows, points)
+def cross_rows(designs, root_weights, points, stacked_points, cross_ref):
+    rows, kernel = kernel_values(designs * root_weights, points, stacked_points)
     gap_u = gap_along(rows, points, DIM - 2)
     gap_v = gap_along(rows, points, DIM - 1)
     n = rows.shape[0]
@@ -207,65 +224,68 @@
 
 def update_kernel(
     col_ref, own_ref, first_ref, second_ref, roots_ref, inverse_ref, far_ref, trailing_ref,
-    updated_ref, shard_ref, points_ref, root_ref, hi_ref, lo_ref, cross_ref, tiles_ref, sems,
+    updated_ref, shard_ref, tiles_ref, cross_ref, in_sems, out_sems,
 ):
     half = PANEL // 2
-    step = pl.program_id(0)
     steps, _, tile_width = tiles_ref.shape
 
-    def tile_copy(j):
-        columns = trailing_ref.at[:, pl.ds(pl.multiple_of(j * tile_width, 128), tile_width)]
-        return pltpu.make_async_copy(columns, tiles_ref.at[j], sems.at[j])
-
-    @pl.when(step == 0)
-    def _():
-        for j in range(steps):
-            tile_copy(j).start()
-        root_ref[...] = roots_column(roots_ref)
-        points_ref[...] = jnp.concatenate([first_ref[...], second_ref[...]], 1) * root_ref[...]
-        cross = cross_rows(own_ref[...], root_ref[...], points_ref[...], cross_ref)
-        left = dot_nt(cross[:, :half], inverse_ref[:half, :half])
-        right = dot_nt(cross, inverse_ref[half:, :])
-        left_hi, left_lo = split(left)
-        right_hi, right_lo = split(right)
-        rows_hi = jnp.concatenate([left_hi, right_hi], 1)
-        rows_lo = jnp.concatenate([left_lo, right_lo], 1)
-        width = shard_ref.shape[0]
-        chosen = lax.broadcasted_iota(jnp.int32, (width, PANEL), 0) + col_ref[0] * width
-        pick = jnp.where(lax.broadcasted_iota(jnp.int32, (width, PANEL), 1) == chosen, 1.0, 0.0).astype(BF16)
-        shard_ref[...] = dot_one(pick, rows_hi, NT) + dot_one(pick, rows_lo, NT)
-        inv_hi, inv_lo = split(inverse_ref[...])
-        left = dot_split((rows_hi, rows_lo), (inv_hi[:, :half], inv_lo[:, :half]), NN)
-        right = dot_split((right_hi, right_lo), (inv_hi[half:, half:], inv_lo[half:, half:]), NN)
-        hi_ref[:, :half], lo_ref[:, :half] = split(left)
-        hi_ref[:, half:], lo_ref[:, half:] = split(right)
-
-    far = split(cross_rows(far_ref[0], root_ref[...], points_ref[...], cross_ref))
-    product = dot_split((hi_ref[...], lo_ref[...]), far)
-    tile_copy(step).wait()
-    updated_ref[...] = tiles_ref[step] - product
+    def columns(ref, j):
+        return ref.at[:, j * tile_width : (j + 1) * tile_width]
+
+    arrive = [pltpu.make_async_copy(columns(trailing_ref, j), tiles_ref.at[j], in_sems.at[j]) for j in range(steps)]
+    leave = [pltpu.make_async_copy(tiles_ref.at[j], columns(updated_ref, j), out_sems.at[j]) for j in range(steps)]
+    for copy in arrive:
+        copy.start()
+
+    roots = roots_column(roots_ref)
+    points = jnp.concatenate([first_ref[...], second_ref[...]], 1) * roots
+    stacked = stack_right(points)
+    cross = cross_rows(own_ref[...], roots, points, stacked, cross_ref.at[steps])
+    left = dot_nt(cross[:, :half], inverse_ref[:half, :half])
+    right = dot_nt(cross, inverse_ref[half:, :])
+    left_hi, left_lo = split(left)
+    right_hi, right_lo = split(right)
+    rows_hi = jnp.concatenate([left_hi, right_hi], 1)
+    rows_lo = jnp.concatenate([left_lo, right_lo], 1)
+    width = shard_ref.shape[0]
+    chosen = lax.broadcasted_iota(jnp.int32, (width, PANEL), 0) + col_ref[0] * width
+    pick = jnp.where(lax.broadcasted_iota(jnp.int32, (width, PANEL), 1) == chosen, 1.0, 0.0).astype(BF16)
+    shard_ref[...] = dot_one(pick, rows_hi, NT) + dot_one(pick, rows_lo, NT)
+    inv_hi, inv_lo = split(inverse_ref[...])
+    left = dot_split((rows_hi, rows_lo), (inv_hi[:, :half], inv_lo[:, :half]), NN)
+    right = dot_split((right_hi, right_lo), (inv_hi[half:, half:], inv_lo[half:, half:]), NN)
+    left_hi, left_lo = split(left)
+    right_hi, right_lo = split(right)
+    rows = (jnp.concatenate([left_hi, right_hi], 1), jnp.concatenate([left_lo, right_lo], 1))
+
+    far = split(cross_rows(far_ref[0], roots, points, stacked, cross_ref.at[0]))
+    for copy in arrive:
+        copy.wait()
+    for j in range(steps):
+        here = far
+        if j + 1 < steps:
+            far = split(cross_rows(far_ref[j + 1], roots, points, stacked, cross_ref.at[j + 1]))
+        tiles_ref[j] = tiles_ref[j] - dot_split(rows, here)
+        leave[j].start()
+    for copy in leave:
+        copy.wait()
 
 
 def update_call(col, panel_width, own, first, second, roots, inverse, far, trailing):
     n = own.shape[1]
     height, width = trailing.shape
     steps = far.shape[0]
-    tile = pl.BlockSpec((height, width // steps), lambda j: (0, j))
+    in_hbm = pl.BlockSpec(memory_space=pltpu.HBM)
     return pl.pallas_call(
         update_kernel,
-        grid=(steps,),
-        in_specs=[
-            IN_SMEM, IN_VMEM, IN_VMEM, IN_VMEM, IN_VMEM, IN_VMEM, pl.BlockSpec((1, DIM, n), lambda j: (j, 0, 0)),
-            pl.BlockSpec(memory_space=pltpu.HBM),
-        ],
-        out_specs=[tile, pl.BlockSpec((panel_width, height), lambda j: (0, 0))],
+        in_specs=[IN_SMEM] + [IN_VMEM] * 6 + [in_hbm],
+        out_specs=[in_hbm, IN_VMEM],
         out_shape=[jax.ShapeDtypeStruct((height, width), F32), jax.ShapeDtypeStruct((panel_width, height), F32)],
         scratch_shapes=[
-            pltpu.VMEM((DIM, PANEL), F32), pltpu.VMEM((DIM, 1), F32), pltpu.VMEM((height, PANEL), BF16),
-            pltpu.VMEM((height, PANEL), BF16), pltpu.VMEM((PANEL // 128, 2 * n, 128), F32),
-            pltpu.VMEM((steps, height, width // steps), F32), pltpu.SemaphoreType.DMA((steps,)),
+            pltpu.VMEM((steps, height, width // steps), F32), pltpu.VMEM((steps + 1, PANEL // 128, 2 * n, 128), F32),
+            pltpu.SemaphoreType.DMA((steps,)), pltpu.SemaphoreType.DMA((steps,)),
         ],
-        compiler_params=pltpu.CompilerParams(vmem_limit_bytes=48 << 20, dimension_semantics=("arbitrary",)),
+        compiler_params=pltpu.CompilerParams(vmem_limit_bytes=40 << 20),
         name="trailing_update",
     )(col, own, first, second, roots, inverse, far, pltpu.with_memory_space_constraint(trailing, pltpu.HBM))
 
@@ -299,6 +319,8 @@
         return chosen
 
     from_x = rounds(designs, along_x)
+    one = jnp.where(at >= 0, 1.0, 2.0).astype(F32)
+    from_x[0] = lax.optimization_barrier(designs * one)
     block_of = lambda x: pick(from_x, (x_at - x) % NX)
     panel, roots = lax.optimization_barrier((block_of(NX - 1), roots))
     panel = pick(rounds(panel, along_y), (y_at - (NY - 1)) % NY)
@@ -312,14 +334,13 @@
     far = far.reshape(2 * NC, *designs.shape)
     first, second, far = lax.optimization_barrier((first, second, far))
     far = pick(rounds(far, along_y), (y_at - col // 2) % NY)
-    return first, second, far, roots
+    return from_x[0], first, second, far, roots
 
 
 def body(designs, length_weights, trailing):
     width = PANEL // lax.axis_size("pcol")
     col = lax.axis_index("pcol").reshape(1)
-    own = designs.T
-    first, second, far, roots = gather_designs(own, jnp.sqrt(length_weights).reshape(1, DIM))
+    own, first, second, far, roots = gather_designs(designs.T, jnp.sqrt(length_weights).reshape(1, DIM))
     factor_shard, inverse = factor_call(col, width, first, second, roots)
     updated, rows_shard = update_call(col, width, own, first, second, roots, inverse, far, trailing)
     return updated, rows_shard.T, factor_shard.T

time: 55.2 us -> 53.8 us (0.975)
  Pallas kernels: 29.6 us -> 27.9 us
    pallas_call x1, Pallas kernels: 13 us -> 11.5 us  [update_call(): pl.pallas_call(update_kernel, in_specs=[IN_SMEM] + [IN_VMEM] * 6 + [in_hb...]
    mul x0 -> x1, other arithmetic: none -> 0.88 us  [gather_designs(): from_x[0] = lax.optimization_barrier(designs * one)]
    another operation x2, other arithmetic: 0.88 us -> 0.04 us  [gather_designs(): far = jnp.stack([block_of(half), block_of(half + 1)], 0)]
  transfers between devices with their start and end apart: 11 -> 11, of which waited for: 3 -> 3; matrix products, arithmetic and copies ran while one was open for 1% -> 3% of each run, Pallas kernels for 31% -> 31%
where the time goes in v3:
time: 53.8 us; the launch traced here: 52.8 us
  Pallas kernels  27.9 us (52%)
  starting transfers between devices  19.1 us (36%)
  waiting for transfers between devices  3.23 us (6%)
  other arithmetic  1.05 us (2%)
  between operations  0.88 us (2%)
  local copies, waits for them, and re-layouts  0.68 us (1%)
    ppermute x11, starting transfers between devices, gather_designs(): send = lambda block, pairs: lax.ppermute(block, 'prow', pairs)  19.1 us
    pallas_call x1, Pallas kernels, factor_call(): pl.pallas_call(factor_kernel, in_specs=[IN_SMEM, IN_VMEM, IN_VMEM, IN_VME...  16.4 us
    pallas_call x1, Pallas kernels, update_call(): pl.pallas_call(update_kernel, in_specs=[IN_SMEM] + [IN_VMEM] * 6 + [in_hb...  11.5 us
    ppermute x11, waiting for transfers between devices, gather_designs(): send = lambda block, pairs: lax.ppermute(block, 'prow', pairs)  3.23 us
  transfers between devices with their start and end apart: 11, of which 3 were waited for; matrix products, arithmetic and copies ran while one was open for 3% of the time, Pallas kernels for 31%

profile of v3, /device:TPU:65, one launch (start us, length us, event | category | flops | bytes accessed | tf_op | source)
XLA Modules:
  0.0 52.8 jit_solution(13929975945474825018)
XLA Ops:
  0.6 2.8 %collective-permute-start.1 = (f32[64,256]{1,0:T(8,128)}, f32[64,256]{1,0:T(8,128)S(1)}, u32[]{:S(2)}, u32[]{:S(2)}) collective-permute-start(f32[64,256]{1,0:T(8,128)} %bitcast.20), channel_id=1, source_target_pairs={{0,32},{8,40},{16,48},{24,56},{32,0},{40,8},{48,16},{56,24},{64,96... | collective-permute-start | bytes 196616 | tf_op jit(solution)/shard_map/ppermute | solution.py:309
  3.5 0.9 %collective-permute-start = (f32[64,256]{1,0:T(8,128)}, f32[64,256]{1,0:T(8,128)S(1)}, u32[]{:S(2)}, u32[]{:S(2)}) collective-permute-start(f32[64,256]{1,0:T(8,128)} %bitcast.21), channel_id=1, source_target_pairs={{0,48},{8,56},{16,0},{24,8},{32,16},{40,24},{48,32},{56,40},{64,11... | collective-permute-start | bytes 196616 | tf_op jit(solution)/shard_map/ppermute | solution.py:309
  4.3 0.6 %collective-permute-start.2 = (f32[64,256]{1,0:T(8,128)}, f32[64,256]{1,0:T(8,128)S(1)}, u32[]{:S(2)}, u32[]{:S(2)}) collective-permute-start(f32[64,256]{1,0:T(8,128)} %bitcast.22), channel_id=1, source_target_pairs={{0,16},{8,24},{16,32},{24,40},{32,48},{40,56},{48,0},{56,8},{64,80... | collective-permute-start | bytes 196616 | tf_op jit(solution)/shard_map/ppermute | solution.py:309
  4.9 0.9 %broadcast_multiply_fusion.own_ref = f32[64,256]{1,0:T(8,128)S(1)} fusion(f32[]{:T(128)S(6)} %select_n.165, f32[256,64]{0,1:T(8,128)} %param.3), kind=kLoop, calls=%fused_computation.9 | loop fusion | flops 16384 | bytes 131076 | tf_op jit(solution)/shard_map/mul | solution.py:323
  5.8 0.7 %sqrt_bitcast_fusion.roots_ref = f32[1,64]{1,0:T(1,128)S(1)} fusion(f32[64]{0:T(128)} %param.4), kind=kLoop, calls=%fused_computation.12 | loop fusion | bytes 512 | tf_op jit(solution)/shard_map/reshape | solution.py:343
  6.5 0.0 collective-permute-done.1
  6.5 1.0 %collective-permute-done = f32[64,256]{1,0:T(8,128)S(1)} collective-permute-done((f32[64,256]{1,0:T(8,128)}, f32[64,256]{1,0:T(8,128)S(1)}, u32[]{:S(2)}, u32[]{:S(2)}) %collective-permute-start) | collective-permute-done | bytes 65568 | tf_op jit(solution)/shard_map/ppermute | solution.py:309
  7.5 1.4 %collective-permute-done.2 = f32[64,256]{1,0:T(8,128)S(1)} collective-permute-done((f32[64,256]{1,0:T(8,128)}, f32[64,256]{1,0:T(8,128)S(1)}, u32[]{:S(2)}, u32[]{:S(2)}) %collective-permute-start.2) | collective-permute-done | bytes 65568 | tf_op jit(solution)/shard_map/ppermute | solution.py:309
  8.9 1.4 %collective-permute-start.5 = (f32[64,256]{1,0:T(8,128)S(1)}, f32[64,256]{1,0:T(8,128)S(1)}, u32[]{:S(2)}, u32[]{:S(2)}) collective-permute-start(f32[64,256]{1,0:T(8,128)S(1)} %get-tuple-element.12), channel_id=1, source_target_pairs={{0,64},{8,72},{16,80},{24,88},{32,96},{40,104},{48,112},{56,120},{... | collective-permute-start | bytes 196616 | tf_op jit(solution)/shard_map/ppermute | solution.py:309
  10.3 2.6 %collective-permute-start.4 = (f32[64,256]{1,0:T(8,128)S(1)}, f32[64,256]{1,0:T(8,128)S(1)}, u32[]{:S(2)}, u32[]{:S(2)}) collective-permute-start(f32[64,256]{1,0:T(8,128)S(1)} %get-tuple-element.12), channel_id=1, source_target_pairs={{0,128},{8,136},{16,144},{24,152},{32,160},{40,168},{48,176},{56,1... | collective-permute-start | bytes 196616 | tf_op jit(solution)/shard_map/ppermute | solution.py:309
  12.9 1.1 %collective-permute-start.3 = (f32[64,256]{1,0:T(8,128)S(1)}, f32[64,256]{1,0:T(8,128)S(1)}, u32[]{:S(2)}, u32[]{:S(2)}) collective-permute-start(f32[64,256]{1,0:T(8,128)S(1)} %get-tuple-element.12), channel_id=1, source_target_pairs={{0,192},{8,200},{16,208},{24,216},{32,224},{40,232},{48,240},{56,2... | collective-permute-start | bytes 196616 | tf_op jit(solution)/shard_map/ppermute | solution.py:309
  14.0 3.3 %collective-permute-start.7 = (f32[2,64,256]{2,1,0:T(8,128)S(1)}, f32[2,64,256]{2,1,0:T(8,128)S(1)}, u32[]{:S(2)}, u32[]{:S(2)}) collective-permute-start(f32[2,64,256]{2,1,0:T(8,128)S(1)} %pad_maximum_fusion.1), channel_id=1, source_target_pairs={{0,8},{8,0},{16,24},{24,16},{32,40},{40,32},{48,56},{56,48},{64,72... | collective-permute-start | bytes 393224 | tf_op jit(solution)/shard_map/ppermute | solution.py:309
  17.3 0.0 collective-permute-done.5
  17.3 0.0 collective-permute-done.4
  17.3 0.0 collective-permute-done.3
  17.3 2.9 %collective-permute-start.6 = (f32[64,256]{1,0:T(8,128)S(1)}, f32[64,256]{1,0:T(8,128)S(1)}, u32[]{:S(2)}, u32[]{:S(2)}) collective-permute-start(f32[64,256]{1,0:T(8,128)S(1)} %select_select_fusion.1), channel_id=1, source_target_pairs={{0,8},{8,0},{16,24},{24,16},{32,40},{40,32},{48,56},{56,48},{64,72... | collective-permute-start | bytes 196616 | tf_op jit(solution)/shard_map/ppermute | solution.py:309
  20.2 0.0 collective-permute-done.7
  20.3 0.8 %collective-permute-done.6 = f32[64,256]{1,0:T(8,128)S(1)} collective-permute-done((f32[64,256]{1,0:T(8,128)S(1)}, f32[64,256]{1,0:T(8,128)S(1)}, u32[]{:S(2)}, u32[]{:S(2)}) %collective-permute-start.6) | collective-permute-done | bytes 65568 | tf_op jit(solution)/shard_map/ppermute | solution.py:309
  21.1 0.1 collective-permute-start.10
  21.2 3.4 %collective-permute-start.9 = (f32[4,64,256]{2,1,0:T(8,128)S(1)}, f32[4,64,256]{2,1,0:T(8,128)S(1)}, u32[]{:S(2)}, u32[]{:S(2)}) collective-permute-start(f32[4,64,256]{2,1,0:T(8,128)S(1)} %bitcast.17), channel_id=1, source_target_pairs={{0,128},{8,136},{16,144},{24,152},{32,160},{40,168},{48,176},{56,1... | collective-permute-start | bytes 786440 | tf_op jit(solution)/shard_map/ppermute | solution.py:309
  24.7 0.0 collective-permute-start.8
  24.7 16.4 %panel_factor.1 = (f32[64,512]{1,0:T(8,128)}, f32[512,512]{1,0:T(8,128)S(1)}) custom-call(s32[1]{0:T(128)} %bitcast.col_ref, f32[64,256]{1,0:T(8,128)S(1)} %get-tuple-element.13.first_ref, f32[64,256]{1,0:T(8,128)S(1)} %get-tuple-element.14.second_ref, f32[1,64]{1,0:T(1,128)S(1)} %sqrt_bitcast_fusion.roots_ref), custom_call_target="tpu_custom_call" | custom-call | tf_op jit(solution)/shard_map/panel_factor/pallas_call | solution.py:199
  41.1 0.0 collective-permute-done.10
  41.1 0.0 collective-permute-done.9
  41.1 0.0 collective-permute-done.8
  41.1 0.1 select_select_fusion.far_ref
  41.2 11.5 %trailing_update.1 = (f32[512,2048]{1,0:T(8,128)}, f32[64,512]{1,0:T(8,128)}) custom-call(s32[1]{0:T(128)} %bitcast.col_ref, f32[64,256]{1,0:T(8,128)S(1)} %broadcast_multiply_fusion.own_ref, f32[64,256]{1,0:T(8,128)S(1)} %get-tuple-element.13.first_ref, f32[64,256]{1,0:T(8,128)S(1)} %get-tuple-element.14.second_ref, ...), custom_call_target="tpu_custom_call" | custom-call | tf_op jit(solution)/shard_map/trailing_update/pallas_call | solution.py:279
  (7 shorter events, 0.1 us)
Async XLA Ops:
  0.6 5.8 %collective-permute-start.1 = (f32[64,256]{1,0:T(8,128)}, f32[64,256]{1,0:T(8,128)S(1)}, u32[]{:S(2)}, u32[]{:S(2)}) collective-permute-start(f32[64,256]{1,0:T(8,128)} %bitcast.20), channel_id=1, source_target_pairs={{0,32},{8,40},{16,48},{24,56},{32,0},{40,8},{48,16},{56,24},{64,96... | collective-permute-start | bytes 196616 | tf_op jit(solution)/shard_map/ppermute | solution.py:309
  3.5 4.0 %collective-permute-start = (f32[64,256]{1,0:T(8,128)}, f32[64,256]{1,0:T(8,128)S(1)}, u32[]{:S(2)}, u32[]{:S(2)}) collective-permute-start(f32[64,256]{1,0:T(8,128)} %bitcast.21), channel_id=1, source_target_pairs={{0,48},{8,56},{16,0},{24,8},{32,16},{40,24},{48,32},{56,40},{64,11... | collective-permute-start | bytes 196616 | tf_op jit(solution)/shard_map/ppermute | solution.py:309
  4.3 4.5 %collective-permute-start.2 = (f32[64,256]{1,0:T(8,128)}, f32[64,256]{1,0:T(8,128)S(1)}, u32[]{:S(2)}, u32[]{:S(2)}) collective-permute-start(f32[64,256]{1,0:T(8,128)} %bitcast.22), channel_id=1, source_target_pairs={{0,16},{8,24},{16,32},{24,40},{32,48},{40,56},{48,0},{56,8},{64,80... | collective-permute-start | bytes 196616 | tf_op jit(solution)/shard_map/ppermute | solution.py:309
  8.9 8.4 %collective-permute-start.5 = (f32[64,256]{1,0:T(8,128)S(1)}, f32[64,256]{1,0:T(8,128)S(1)}, u32[]{:S(2)}, u32[]{:S(2)}) collective-permute-start(f32[64,256]{1,0:T(8,128)S(1)} %get-tuple-element.12), channel_id=1, source_target_pairs={{0,64},{8,72},{16,80},{24,88},{32,96},{40,104},{48,112},{56,120},{... | collective-permute-start | bytes 196616 | tf_op jit(solution)/shard_map/ppermute | solution.py:309
  10.3 7.0 %collective-permute-start.4 = (f32[64,256]{1,0:T(8,128)S(1)}, f32[64,256]{1,0:T(8,128)S(1)}, u32[]{:S(2)}, u32[]{:S(2)}) collective-permute-start(f32[64,256]{1,0:T(8,128)S(1)} %get-tuple-element.12), channel_id=1, source_target_pairs={{0,128},{8,136},{16,144},{24,152},{32,160},{40,168},{48,176},{56,1... | collective-permute-start | bytes 196616 | tf_op jit(solution)/shard_map/ppermute | solution.py:309
  12.9 4.4 %collective-permute-start.3 = (f32[64,256]{1,0:T(8,128)S(1)}, f32[64,256]{1,0:T(8,128)S(1)}, u32[]{:S(2)}, u32[]{:S(2)}) collective-permute-start(f32[64,256]{1,0:T(8,128)S(1)} %get-tuple-element.12), channel_id=1, source_target_pairs={{0,192},{8,200},{16,208},{24,216},{32,224},{40,232},{48,240},{56,2... | collective-permute-start | bytes 196616 | tf_op jit(solution)/shard_map/ppermute | solution.py:309
  14.0 6.2 %collective-permute-start.7 = (f32[2,64,256]{2,1,0:T(8,128)S(1)}, f32[2,64,256]{2,1,0:T(8,128)S(1)}, u32[]{:S(2)}, u32[]{:S(2)}) collective-permute-start(f32[2,64,256]{2,1,0:T(8,128)S(1)} %pad_maximum_fusion.1), channel_id=1, source_target_pairs={{0,8},{8,0},{16,24},{24,16},{32,40},{40,32},{48,56},{56,48},{64,72... | collective-permute-start | bytes 393224 | tf_op jit(solution)/shard_map/ppermute | solution.py:309
  17.3 3.8 %collective-permute-start.6 = (f32[64,256]{1,0:T(8,128)S(1)}, f32[64,256]{1,0:T(8,128)S(1)}, u32[]{:S(2)}, u32[]{:S(2)}) collective-permute-start(f32[64,256]{1,0:T(8,128)S(1)} %select_select_fusion.1), channel_id=1, source_target_pairs={{0,8},{8,0},{16,24},{24,16},{32,40},{40,32},{48,56},{56,48},{64,72... | collective-permute-start | bytes 196616 | tf_op jit(solution)/shard_map/ppermute | solution.py:309
  21.1 20.0 %collective-permute-start.10 = (f32[4,64,256]{2,1,0:T(8,128)S(1)}, f32[4,64,256]{2,1,0:T(8,128)S(1)}, u32[]{:S(2)}, u32[]{:S(2)}) collective-permute-start(f32[4,64,256]{2,1,0:T(8,128)S(1)} %bitcast.16), channel_id=1, source_target_pairs={{0,64},{8,72},{16,80},{24,88},{32,96},{40,104},{48,112},{56,120},{... | collective-permute-start | bytes 786440 | tf_op jit(solution)/shard_map/ppermute | solution.py:309
  21.2 19.9 %collective-permute-start.9 = (f32[4,64,256]{2,1,0:T(8,128)S(1)}, f32[4,64,256]{2,1,0:T(8,128)S(1)}, u32[]{:S(2)}, u32[]{:S(2)}) collective-permute-start(f32[4,64,256]{2,1,0:T(8,128)S(1)} %bitcast.17), channel_id=1, source_target_pairs={{0,128},{8,136},{16,144},{24,152},{32,160},{40,168},{48,176},{56,1... | collective-permute-start | bytes 786440 | tf_op jit(solution)/shard_map/ppermute | solution.py:309
  24.7 16.5 %collective-permute-start.8 = (f32[4,64,256]{2,1,0:T(8,128)S(1)}, f32[4,64,256]{2,1,0:T(8,128)S(1)}, u32[]{:S(2)}, u32[]{:S(2)}) collective-permute-start(f32[4,64,256]{2,1,0:T(8,128)S(1)} %bitcast.18), channel_id=1, source_target_pairs={{0,192},{8,200},{16,208},{24,216},{32,224},{40,232},{48,240},{56,2... | collective-permute-start | bytes 786440 | tf_op jit(solution)/shard_map/ppermute | solution.py:309

commit v4 on v3

--- a/solution.py
+++ b/solution.py
@@ -172,7 +172,10 @@
                 end = BLOCK * (s + 1)
                 below = dot_nt(work_ref[end:, end - BLOCK : end], inverse)
                 factor_ref[end:, end - BLOCK : end] = below
-                work_ref[end:, end:] = work_ref[end:, end:] - dot_nt(below, below)
+                for t in range(0, PANEL - end, BLOCK):
+                    top = end + t
+                    product = dot_nt(below[t:], below[t : t + BLOCK])
+                    work_ref[top:, top : top + BLOCK] = work_ref[top:, top : top + BLOCK] - product
 
     for n in (BLOCK, 2 * BLOCK):
         for t in range(0, PANEL, 2 * n):

time: 53.8 us -> 53.5 us (level)
  no operation moved by 1% of the time
where the time goes in v4:
time: 53.5 us; the launch traced here: 52.6 us
  Pallas kernels  27.6 us (52%)
  starting transfers between devices  19.1 us (36%)
  waiting for transfers between devices  3.23 us (6%)
  other arithmetic  1.05 us (2%)
  between operations  0.88 us (2%)
  local copies, waits for them, and re-layouts  0.68 us (1%)
    ppermute x11, starting transfers between devices, gather_designs(): send = lambda block, pairs: lax.ppermute(block, 'prow', pairs)  19.1 us
    pallas_call x1, Pallas kernels, factor_call(): pl.pallas_call(factor_kernel, in_specs=[IN_SMEM, IN_VMEM, IN_VMEM, IN_VME...  16.2 us
    pallas_call x1, Pallas kernels, update_call(): pl.pallas_call(update_kernel, in_specs=[IN_SMEM] + [IN_VMEM] * 6 + [in_hb...  11.5 us
    ppermute x11, waiting for transfers between devices, gather_designs(): send = lambda block, pairs: lax.ppermute(block, 'prow', pairs)  3.23 us
  transfers between devices with their start and end apart: 11, of which 3 were waited for; matrix products, arithmetic and copies ran while one was open for 3% of the time, Pallas kernels for 31%

profile of v4, /device:TPU:65, one launch (start us, length us, event | category | flops | bytes accessed | tf_op | source)
XLA Modules:
  0.0 52.6 jit_solution(5579130844675169091)
XLA Ops:
  0.6 2.8 %collective-permute-start.1 = (f32[64,256]{1,0:T(8,128)}, f32[64,256]{1,0:T(8,128)S(1)}, u32[]{:S(2)}, u32[]{:S(2)}) collective-permute-start(f32[64,256]{1,0:T(8,128)} %bitcast.20), channel_id=1, source_target_pairs={{0,32},{8,40},{16,48},{24,56},{32,0},{40,8},{48,16},{56,24},{64,96... | collective-permute-start | bytes 196616 | tf_op jit(solution)/shard_map/ppermute | solution.py:312
  3.5 0.9 %collective-permute-start = (f32[64,256]{1,0:T(8,128)}, f32[64,256]{1,0:T(8,128)S(1)}, u32[]{:S(2)}, u32[]{:S(2)}) collective-permute-start(f32[64,256]{1,0:T(8,128)} %bitcast.21), channel_id=1, source_target_pairs={{0,48},{8,56},{16,0},{24,8},{32,16},{40,24},{48,32},{56,40},{64,11... | collective-permute-start | bytes 196616 | tf_op jit(solution)/shard_map/ppermute | solution.py:312
  4.3 0.6 %collective-permute-start.2 = (f32[64,256]{1,0:T(8,128)}, f32[64,256]{1,0:T(8,128)S(1)}, u32[]{:S(2)}, u32[]{:S(2)}) collective-permute-start(f32[64,256]{1,0:T(8,128)} %bitcast.22), channel_id=1, source_target_pairs={{0,16},{8,24},{16,32},{24,40},{32,48},{40,56},{48,0},{56,8},{64,80... | collective-permute-start | bytes 196616 | tf_op jit(solution)/shard_map/ppermute | solution.py:312
  4.9 0.9 %broadcast_multiply_fusion.own_ref = f32[64,256]{1,0:T(8,128)S(1)} fusion(f32[]{:T(128)S(6)} %select_n.165, f32[256,64]{0,1:T(8,128)} %param.3), kind=kLoop, calls=%fused_computation.9 | loop fusion | flops 16384 | bytes 131076 | tf_op jit(solution)/shard_map/mul | solution.py:326
  5.8 0.7 %sqrt_bitcast_fusion.roots_ref = f32[1,64]{1,0:T(1,128)S(1)} fusion(f32[64]{0:T(128)} %param.4), kind=kLoop, calls=%fused_computation.12 | loop fusion | bytes 512 | tf_op jit(solution)/shard_map/reshape | solution.py:346
  6.5 0.0 collective-permute-done.1
  6.5 1.0 %collective-permute-done = f32[64,256]{1,0:T(8,128)S(1)} collective-permute-done((f32[64,256]{1,0:T(8,128)}, f32[64,256]{1,0:T(8,128)S(1)}, u32[]{:S(2)}, u32[]{:S(2)}) %collective-permute-start) | collective-permute-done | bytes 65568 | tf_op jit(solution)/shard_map/ppermute | solution.py:312
  7.5 1.4 %collective-permute-done.2 = f32[64,256]{1,0:T(8,128)S(1)} collective-permute-done((f32[64,256]{1,0:T(8,128)}, f32[64,256]{1,0:T(8,128)S(1)}, u32[]{:S(2)}, u32[]{:S(2)}) %collective-permute-start.2) | collective-permute-done | bytes 65568 | tf_op jit(solution)/shard_map/ppermute | solution.py:312
  8.9 1.4 %collective-permute-start.5 = (f32[64,256]{1,0:T(8,128)S(1)}, f32[64,256]{1,0:T(8,128)S(1)}, u32[]{:S(2)}, u32[]{:S(2)}) collective-permute-start(f32[64,256]{1,0:T(8,128)S(1)} %get-tuple-element.12), channel_id=1, source_target_pairs={{0,64},{8,72},{16,80},{24,88},{32,96},{40,104},{48,112},{56,120},{... | collective-permute-start | bytes 196616 | tf_op jit(solution)/shard_map/ppermute | solution.py:312
  10.3 2.6 %collective-permute-start.4 = (f32[64,256]{1,0:T(8,128)S(1)}, f32[64,256]{1,0:T(8,128)S(1)}, u32[]{:S(2)}, u32[]{:S(2)}) collective-permute-start(f32[64,256]{1,0:T(8,128)S(1)} %get-tuple-element.12), channel_id=1, source_target_pairs={{0,128},{8,136},{16,144},{24,152},{32,160},{40,168},{48,176},{56,1... | collective-permute-start | bytes 196616 | tf_op jit(solution)/shard_map/ppermute | solution.py:312
  12.9 1.1 %collective-permute-start.3 = (f32[64,256]{1,0:T(8,128)S(1)}, f32[64,256]{1,0:T(8,128)S(1)}, u32[]{:S(2)}, u32[]{:S(2)}) collective-permute-start(f32[64,256]{1,0:T(8,128)S(1)} %get-tuple-element.12), channel_id=1, source_target_pairs={{0,192},{8,200},{16,208},{24,216},{32,224},{40,232},{48,240},{56,2... | collective-permute-start | bytes 196616 | tf_op jit(solution)/shard_map/ppermute | solution.py:312
  14.0 3.3 %collective-permute-start.7 = (f32[2,64,256]{2,1,0:T(8,128)S(1)}, f32[2,64,256]{2,1,0:T(8,128)S(1)}, u32[]{:S(2)}, u32[]{:S(2)}) collective-permute-start(f32[2,64,256]{2,1,0:T(8,128)S(1)} %pad_maximum_fusion.1), channel_id=1, source_target_pairs={{0,8},{8,0},{16,24},{24,16},{32,40},{40,32},{48,56},{56,48},{64,72... | collective-permute-start | bytes 393224 | tf_op jit(solution)/shard_map/ppermute | solution.py:312
  17.3 0.0 collective-permute-done.5
  17.3 0.0 collective-permute-done.4
  17.3 0.0 collective-permute-done.3
  17.3 2.9 %collective-permute-start.6 = (f32[64,256]{1,0:T(8,128)S(1)}, f32[64,256]{1,0:T(8,128)S(1)}, u32[]{:S(2)}, u32[]{:S(2)}) collective-permute-start(f32[64,256]{1,0:T(8,128)S(1)} %select_select_fusion.1), channel_id=1, source_target_pairs={{0,8},{8,0},{16,24},{24,16},{32,40},{40,32},{48,56},{56,48},{64,72... | collective-permute-start | bytes 196616 | tf_op jit(solution)/shard_map/ppermute | solution.py:312
  20.2 0.0 collective-permute-done.7
  20.3 0.8 %collective-permute-done.6 = f32[64,256]{1,0:T(8,128)S(1)} collective-permute-done((f32[64,256]{1,0:T(8,128)S(1)}, f32[64,256]{1,0:T(8,128)S(1)}, u32[]{:S(2)}, u32[]{:S(2)}) %collective-permute-start.6) | collective-permute-done | bytes 65568 | tf_op jit(solution)/shard_map/ppermute | solution.py:312
  21.1 0.1 collective-permute-start.10
  21.2 3.4 %collective-permute-start.9 = (f32[4,64,256]{2,1,0:T(8,128)S(1)}, f32[4,64,256]{2,1,0:T(8,128)S(1)}, u32[]{:S(2)}, u32[]{:S(2)}) collective-permute-start(f32[4,64,256]{2,1,0:T(8,128)S(1)} %bitcast.17), channel_id=1, source_target_pairs={{0,128},{8,136},{16,144},{24,152},{32,160},{40,168},{48,176},{56,1... | collective-permute-start | bytes 786440 | tf_op jit(solution)/shard_map/ppermute | solution.py:312
  24.7 0.0 collective-permute-start.8
  24.7 16.2 %panel_factor.1 = (f32[64,512]{1,0:T(8,128)}, f32[512,512]{1,0:T(8,128)S(1)}) custom-call(s32[1]{0:T(128)} %bitcast.col_ref, f32[64,256]{1,0:T(8,128)S(1)} %get-tuple-element.13.first_ref, f32[64,256]{1,0:T(8,128)S(1)} %get-tuple-element.14.second_ref, f32[1,64]{1,0:T(1,128)S(1)} %sqrt_bitcast_fusion.roots_ref), custom_call_target="tpu_custom_call" | custom-call | tf_op jit(solution)/shard_map/panel_factor/pallas_call | solution.py:202
  40.8 0.0 collective-permute-done.10
  40.8 0.0 collective-permute-done.9
  40.8 0.0 collective-permute-done.8
  40.8 0.1 select_select_fusion.far_ref
  40.9 11.5 %trailing_update.1 = (f32[512,2048]{1,0:T(8,128)}, f32[64,512]{1,0:T(8,128)}) custom-call(s32[1]{0:T(128)} %bitcast.col_ref, f32[64,256]{1,0:T(8,128)S(1)} %broadcast_multiply_fusion.own_ref, f32[64,256]{1,0:T(8,128)S(1)} %get-tuple-element.13.first_ref, f32[64,256]{1,0:T(8,128)S(1)} %get-tuple-element.14.second_ref, ...), custom_call_target="tpu_custom_call" | custom-call | tf_op jit(solution)/shard_map/trailing_update/pallas_call | solution.py:282
  (7 shorter events, 0.1 us)
Async XLA Ops:
  0.6 5.8 %collective-permute-start.1 = (f32[64,256]{1,0:T(8,128)}, f32[64,256]{1,0:T(8,128)S(1)}, u32[]{:S(2)}, u32[]{:S(2)}) collective-permute-start(f32[64,256]{1,0:T(8,128)} %bitcast.20), channel_id=1, source_target_pairs={{0,32},{8,40},{16,48},{24,56},{32,0},{40,8},{48,16},{56,24},{64,96... | collective-permute-start | bytes 196616 | tf_op jit(solution)/shard_map/ppermute | solution.py:312
  3.5 4.0 %collective-permute-start = (f32[64,256]{1,0:T(8,128)}, f32[64,256]{1,0:T(8,128)S(1)}, u32[]{:S(2)}, u32[]{:S(2)}) collective-permute-start(f32[64,256]{1,0:T(8,128)} %bitcast.21), channel_id=1, source_target_pairs={{0,48},{8,56},{16,0},{24,8},{32,16},{40,24},{48,32},{56,40},{64,11... | collective-permute-start | bytes 196616 | tf_op jit(solution)/shard_map/ppermute | solution.py:312
  4.3 4.5 %collective-permute-start.2 = (f32[64,256]{1,0:T(8,128)}, f32[64,256]{1,0:T(8,128)S(1)}, u32[]{:S(2)}, u32[]{:S(2)}) collective-permute-start(f32[64,256]{1,0:T(8,128)} %bitcast.22), channel_id=1, source_target_pairs={{0,16},{8,24},{16,32},{24,40},{32,48},{40,56},{48,0},{56,8},{64,80... | collective-permute-start | bytes 196616 | tf_op jit(solution)/shard_map/ppermute | solution.py:312
  8.9 8.4 %collective-permute-start.5 = (f32[64,256]{1,0:T(8,128)S(1)}, f32[64,256]{1,0:T(8,128)S(1)}, u32[]{:S(2)}, u32[]{:S(2)}) collective-permute-start(f32[64,256]{1,0:T(8,128)S(1)} %get-tuple-element.12), channel_id=1, source_target_pairs={{0,64},{8,72},{16,80},{24,88},{32,96},{40,104},{48,112},{56,120},{... | collective-permute-start | bytes 196616 | tf_op jit(solution)/shard_map/ppermute | solution.py:312
  10.3 7.0 %collective-permute-start.4 = (f32[64,256]{1,0:T(8,128)S(1)}, f32[64,256]{1,0:T(8,128)S(1)}, u32[]{:S(2)}, u32[]{:S(2)}) collective-permute-start(f32[64,256]{1,0:T(8,128)S(1)} %get-tuple-element.12), channel_id=1, source_target_pairs={{0,128},{8,136},{16,144},{24,152},{32,160},{40,168},{48,176},{56,1... | collective-permute-start | bytes 196616 | tf_op jit(solution)/shard_map/ppermute | solution.py:312
  12.9 4.4 %collective-permute-start.3 = (f32[64,256]{1,0:T(8,128)S(1)}, f32[64,256]{1,0:T(8,128)S(1)}, u32[]{:S(2)}, u32[]{:S(2)}) collective-permute-start(f32[64,256]{1,0:T(8,128)S(1)} %get-tuple-element.12), channel_id=1, source_target_pairs={{0,192},{8,200},{16,208},{24,216},{32,224},{40,232},{48,240},{56,2... | collective-permute-start | bytes 196616 | tf_op jit(solution)/shard_map/ppermute | solution.py:312
  14.0 6.2 %collective-permute-start.7 = (f32[2,64,256]{2,1,0:T(8,128)S(1)}, f32[2,64,256]{2,1,0:T(8,128)S(1)}, u32[]{:S(2)}, u32[]{:S(2)}) collective-permute-start(f32[2,64,256]{2,1,0:T(8,128)S(1)} %pad_maximum_fusion.1), channel_id=1, source_target_pairs={{0,8},{8,0},{16,24},{24,16},{32,40},{40,32},{48,56},{56,48},{64,72... | collective-permute-start | bytes 393224 | tf_op jit(solution)/shard_map/ppermute | solution.py:312
  17.3 3.8 %collective-permute-start.6 = (f32[64,256]{1,0:T(8,128)S(1)}, f32[64,256]{1,0:T(8,128)S(1)}, u32[]{:S(2)}, u32[]{:S(2)}) collective-permute-start(f32[64,256]{1,0:T(8,128)S(1)} %select_select_fusion.1), channel_id=1, source_target_pairs={{0,8},{8,0},{16,24},{24,16},{32,40},{40,32},{48,56},{56,48},{64,72... | collective-permute-start | bytes 196616 | tf_op jit(solution)/shard_map/ppermute | solution.py:312
  21.1 19.7 %collective-permute-start.10 = (f32[4,64,256]{2,1,0:T(8,128)S(1)}, f32[4,64,256]{2,1,0:T(8,128)S(1)}, u32[]{:S(2)}, u32[]{:S(2)}) collective-permute-start(f32[4,64,256]{2,1,0:T(8,128)S(1)} %bitcast.16), channel_id=1, source_target_pairs={{0,64},{8,72},{16,80},{24,88},{32,96},{40,104},{48,112},{56,120},{... | collective-permute-start | bytes 786440 | tf_op jit(solution)/shard_map/ppermute | solution.py:312
  21.2 19.6 %collective-permute-start.9 = (f32[4,64,256]{2,1,0:T(8,128)S(1)}, f32[4,64,256]{2,1,0:T(8,128)S(1)}, u32[]{:S(2)}, u32[]{:S(2)}) collective-permute-start(f32[4,64,256]{2,1,0:T(8,128)S(1)} %bitcast.17), channel_id=1, source_target_pairs={{0,128},{8,136},{16,144},{24,152},{32,160},{40,168},{48,176},{56,1... | collective-permute-start | bytes 786440 | tf_op jit(solution)/shard_map/ppermute | solution.py:312
  24.7 16.2 %collective-permute-start.8 = (f32[4,64,256]{2,1,0:T(8,128)S(1)}, f32[4,64,256]{2,1,0:T(8,128)S(1)}, u32[]{:S(2)}, u32[]{:S(2)}) collective-permute-start(f32[4,64,256]{2,1,0:T(8,128)S(1)} %bitcast.18), channel_id=1, source_target_pairs={{0,192},{8,200},{16,208},{24,216},{32,224},{40,232},{48,240},{56,2... | collective-permute-start | bytes 786440 | tf_op jit(solution)/shard_map/ppermute | solution.py:312
